TPU v7x, 32 devices: a whole 2x2x4 slice. The times are simulated.
32 devices in a mesh: groups: 2 (over x), ha: 16 (over z, y, core).
Axes of the slice: x: 2, y: 2, z: 4, core: 2. Of those that a mesh axis runs over, the one named last changes fastest.
Arguments:
- video: bfloat16 [8, 64, 192, 192], P('groups', 'ha'), parts along dimension 0, may hold values from -6 to 6
- s1_weight: bfloat16 [3, 3, 192, 128], replicated, may hold values from -0.15625 to 0.15625
- t1_weight: bfloat16 [3, 128, 128], replicated, may hold values from -0.3125 to 0.3125
- r1_weight: bfloat16 [2, 2, 128, 256], replicated, may hold values from -0.25 to 0.25
- s2_weight: bfloat16 [3, 3, 256, 256], replicated, may hold values from -0.125 to 0.125
- t2_weight: bfloat16 [3, 256, 256], replicated, may hold values from -0.21875 to 0.21875
- r2_weight: bfloat16 [2, 2, 256, 512], replicated, may hold values from -0.1875 to 0.1875
- attn_gain: bfloat16 [512], replicated, may hold values from 0.5 to 1.5
- w_query: bfloat16 [512, 512], replicated, may hold values from -2.5 to 2.5
- w_key: bfloat16 [512, 512], replicated, may hold values from -0.27 to 0.27
- w_value: bfloat16 [512, 512], replicated, may hold values from -0.25 to 0.25
- w_out: bfloat16 [512, 512], replicated, may hold values from -1 to 1
Outputs:
- encoded: bfloat16 [8, 16, 48, 512], P('groups', 'ha'), parts along dimension 0
There are 2 independent parts, one for each index of `groups`. A program takes and returns all parts, laid end to end along the dimension named above; an argument that names none is the same for every part. Nothing has to cross between parts.
All inputs are finite; a program needn't handle non-finite values.
Results may differ from a plain program's by a relative error of at most 0.018.
Values may be sent and summed in bfloat16 or wider, within the bound.
No kernel may reach another device: no remote copies, remote signals or barrier semaphores. Data moves between devices by JAX's collectives and lax.ppermute only.
A program may use at most 128 MiB of HBM per device.

v0:
```python
import functools
import math

import jax
import jax.numpy as jnp
from jax import lax
from jax.experimental import pallas as pl
from jax.experimental.pallas import tpu as pltpu
from jax.sharding import PartitionSpec as P


F32 = jnp.float32
BF16 = jnp.bfloat16
AXIS = "ha"
BOTH = ("groups", AXIS)
PHASES = 4


Z_ORDER = (3, 1, 2)
Y_ORDER = (0, 3, 1, 2)


def dot(left, right):
    return jnp.dot(left, right, preferred_element_type=F32)


def turn():
    return lax.axis_index(AXIS) % 2


def whole_row(row, count):
    return row + turn() * (count - 1 - 2 * row)


def inside(far):
    index = lax.axis_index(AXIS)
    at_end = (index == 0) | (index == lax.axis_size(AXIS) - 1)
    return jnp.where(at_end, jnp.zeros_like(far), far)


def causal(a, t_ref, first=0):
    frames, sites, channels = a.shape
    total = None
    for lag in range(3):
        start = max(first - lag, 0)
        held = a[start : frames - lag]
        count = held.shape[0]
        if not count:
            continue
        term = dot(held.reshape(count * sites, channels), t_ref[2 - lag]).reshape(count, sites, -1)
        skip = frames - first - count
        if total is None:
            total = term
        elif skip:
            total = jnp.concatenate([total[:skip], total[skip:] + term], axis=0)
        else:
            total = total + term
    return total


def causal_pairs(a, t_ref, first=0):
    frames, _, channels = a.shape
    none = jnp.zeros_like(t_ref[0])
    results = []
    for frame in range(first, frames, 2):
        held = range(max(frame - 2, 0), frame + 2)

        def tap(source, target):
            lag = target - source
            return t_ref[2 - lag] if 0 <= lag <= 2 else none

        weight = jnp.concatenate(
            [lanes([tap(source, frame), tap(source, frame + 1)]) for source in held], axis=0
        )
        both = dot(lanes([a[source] for source in held]), weight)
        results += [both[:, :channels], both[:, channels:]]
    return jnp.stack(results, axis=0)


def reduction(r_ref):
    first = turn()
    return jnp.concatenate(
        [r_ref[first, 0], r_ref[first, 1], r_ref[1 - first, 0], r_ref[1 - first, 1]], axis=0
    )


def lanes(parts):
    return parts[0] if len(parts) == 1 else jnp.concatenate(parts, axis=-1)


def silu(x):
    return 0.5 * x * (1.0 + jnp.tanh(0.5 * x))


def shifted(x, step, period):
    rows, channels = x.shape
    place = lax.broadcasted_iota(jnp.int32, (rows // period, period, channels), 1)
    place = place.reshape(rows, channels)
    moved = pltpu.roll(x, step % rows, 0)
    return jnp.where(place == (0 if step == 1 else period - 1), 0.0, moved)


def place_phases(total, tap_ref, out_of):
    _, frames, cols, channels = tap_ref.shape
    count = cols // PHASES
    for tap in range(3):
        tap_ref[tap] = total[:, tap * channels : (tap + 1) * channels].reshape(
            frames, cols, channels
        )
    for frame in range(frames):
        def strided(tap, phase):
            return tap_ref[tap, frame, pl.ds(phase, count, stride=PHASES), :]

        for phase in range(PHASES):
            before = (
                shifted(strided(0, PHASES - 1), 1, count)
                if phase == 0
                else strided(0, phase - 1)
            )
            after = (
                shifted(strided(2, 0), -1, count)
                if phase == PHASES - 1
                else strided(2, phase + 1)
            )
            out_of(frame, phase, before + strided(1, phase) + after)


def tap_matrix(w_ref, row):
    return lanes([w_ref[row, tap] for tap in range(3)])


def fetch_rows(video_ref, row, first, rows_to, sem):
    copies = [
        pltpu.make_async_copy(video_ref.at[first + at, row], rows_to.at[at], sem.at[at])
        for at in range(rows_to.shape[0])
    ]
    for copy in copies:
        copy.start()
    return copies


def fetch_taps(w_ref, tap, taps_to, sem):
    copies = [
        pltpu.make_async_copy(w_ref.at[tap, column], taps_to.at[column], sem.at[column])
        for column in range(taps_to.shape[0])
    ]
    for copy in copies:
        copy.start()
    return copies


def finish(copies):
    for copy in copies:
        copy.wait()


def edge_of(rows, taps_ref, tap_ref, out_ref):
    frames, cols, channels = rows.shape
    weight = lanes([taps_ref[column] for column in range(3)])
    total = dot(rows.reshape(frames * cols, channels), weight)

    def store(frame, phase, value):
        out_ref[frame, phase] = value.astype(BF16)

    place_phases(total, tap_ref.at[:, :frames], store)


def first_edge_kernel(video_ref, w_ref, out_ref, rows_to, taps_to, tap_ref, row_sem, tap_sem):
    side = turn()
    row = whole_row(0, video_ref.shape[1])
    copies = fetch_taps(w_ref, 2 - 2 * side, taps_to, tap_sem)
    finish(fetch_rows(video_ref, row, 0, rows_to, row_sem) + copies)
    edge_of(rows_to[...], taps_to, tap_ref, out_ref)


def rest_edge_kernel(video_ref, w_ref, far_out, near_out, tap_ref):
    frames, rows = video_ref.shape[:2]
    side = turn()
    first = frames - far_out.shape[0]
    far = video_ref[first:, whole_row(0, rows)]
    edge_of(far, w_ref.at[2 - 2 * side], tap_ref, far_out)
    edge_of(video_ref[:, whole_row(rows - 1, rows)], w_ref.at[2 * side], tap_ref, near_out)


def inner_rows(wanted, video_ref, w_ref, tap_ref, store_of):
    frames, rows, cols, channels = video_ref.shape
    side = turn()
    taps = {0: 1, -1: 2 * side, 1: 2 - 2 * side}
    totals = {}
    for source in range(max(wanted[0] - 1, 0), min(wanted[-1] + 2, rows)):
        steps = [step for step in taps if source - step in wanted]
        weight = lanes([tap_matrix(w_ref, taps[step]) for step in steps])
        held = video_ref[:, whole_row(source, rows)].reshape(frames * cols, channels)
        terms = dot(held, weight)
        wide = terms.shape[-1] // len(steps)
        for at, step in enumerate(steps):
            term = terms[:, at * wide : (at + 1) * wide]
            row = source - step
            totals[row] = totals[row] + term if row in totals else term
    for row in wanted:
        place_phases(totals[row], tap_ref, store_of(row))


def front_kernel(video_ref, w_ref, t_ref, acc_ref, h_ref, one_ref, tap_ref):
    frames, phases, count, channels = acc_ref.shape

    def store_of(row):
        def store(frame, phase, value):
            if row == 0:
                acc_ref[frame, phase] = value
            else:
                one_ref[frame, phase] = value.astype(BF16)

        return store

    inner_rows((0, 1), video_ref, w_ref, tap_ref, store_of)
    a = one_ref[...].reshape(frames, phases * count, channels)
    h_ref[...] = silu(causal_pairs(a, t_ref)).astype(BF16).reshape(h_ref.shape)


def to_half(h, weight, frames, phases, count):
    return [
        dot(lanes([h(row, 2 * side + j) for row in range(2) for j in range(2)]), weight)
        .astype(BF16)
        .reshape(frames, count, -1)
        for side in range(phases // 2)
    ]


def far_kernel(acc_ref, far_ref, h_in, t_ref, r_ref, *refs, first):
    frames, phases, count, channels = far_ref.shape
    mine = pl.ds(first, frames)
    a = (acc_ref[mine] + inside(far_ref[...].astype(F32))).astype(BF16)
    if first:
        before_ref, d_ref = refs
        whole = jnp.concatenate([before_ref[...], a], axis=0)
    else:
        d_ref, a_ref = refs
        a_ref[...] = a
        whole = a
    whole = whole.reshape(whole.shape[0], phases * count, channels)
    h = silu(causal(whole, t_ref, first)).astype(BF16).reshape(frames, phases, count, channels)
    parts = to_half(
        lambda row, phase: (h_in[mine, phase] if row else h[:, phase]).reshape(
            frames * count, channels
        ),
        reduction(r_ref),
        frames,
        phases,
        count,
    )
    for side, part in enumerate(parts):
        d_ref[:, side] = part


def back_rows_kernel(
    video_ref, w_ref, near_ref, t_ref, r_ref, d_ref, acc_ref, h_ref, tap_ref
):
    frames, phases, count, channels = near_ref.shape
    last = video_ref.shape[1] - 1

    def store_of(row):
        def store(frame, phase, value):
            if row == last:
                value = value + near_ref[frame, phase].astype(F32)
            acc_ref[row - 2, frame, phase] = value.astype(BF16)

        return store

    inner_rows(range(2, last + 1), video_ref, w_ref, tap_ref, store_of)
    for row in range(2, last + 1):
        a = acc_ref[row - 2].reshape(frames, phases * count, channels)
        h_ref[row - 2] = silu(causal(a, t_ref)).astype(BF16).reshape(h_ref.shape[1:])
    weight = reduction(r_ref)
    for half in range(d_ref.shape[0]):
        parts = to_half(
            lambda row, phase: h_ref[2 * half + row, :, phase].reshape(frames * count, channels),
            weight,
            frames,
            phases,
            count,
        )
        for side, part in enumerate(parts):
            d_ref[half, :, side] = part


def place_pairs(total, sites, count, channels):
    even, odd = total[:sites], total[sites:]
    first, middle, last = (slice(tap * channels, (tap + 1) * channels) for tap in range(3))
    return (
        shifted(odd[:, first], 1, count) + even[:, middle] + odd[:, last],
        even[:, first] + odd[:, middle] + shifted(even[:, last], -1, count),
    )


def flat(d):
    frames, sides, count, channels = d.shape
    return jnp.concatenate(
        [d[:, side].reshape(frames * count, channels) for side in range(sides)], axis=0
    )


def by_side(pair, shape):
    frames, _, count, channels = shape
    return jnp.stack([value.reshape(frames, count, channels) for value in pair], axis=1)


def second_rows(a, d, t_ref, first=0):
    _, sides, count, channels = d.shape
    mixed = silu(causal(a.reshape(a.shape[0], sides * count, channels), t_ref, first))
    return (d.astype(F32) + mixed.reshape(d.shape)).astype(BF16)


def middle_kernel(far_a_ref, far_b_ref, rest_ref, near_ref, w_ref, t_ref, acc_ref, h_ref):
    shape = near_ref.shape
    frames, _, count, channels = shape
    sites = frames * count
    rows = rest_ref.shape[0] + 1
    side = turn()
    taps = {-1: 2 * side, 0: 1, 1: 2 - 2 * side}
    held = [jnp.concatenate([far_a_ref[...], far_b_ref[...]], axis=0)]
    held += [rest_ref[row] for row in range(rows - 1)] + [near_ref[...]]
    for row in range(rows):
        total = None
        for step, tap in taps.items():
            if row + step >= 0:
                term = dot(flat(held[row + step]), tap_matrix(w_ref, tap))
                total = term if total is None else total + term
        a = by_side(place_pairs(total, sites, count, channels), shape)
        if row == 0:
            acc_ref[...] = a
        else:
            h_ref[row - 1] = second_rows(a.astype(BF16), held[row], t_ref)


def second_kernel(
    acc_ref, far_ref, d_ref, rest_ref, w_ref, t_ref, r_ref, gain_ref, *refs, first, group_size
):
    shape = d_ref.shape
    frames, _, count, channels = shape
    sites = frames * count
    mine = pl.ds(first, frames)
    more = dot(flat(inside(far_ref[...])), tap_matrix(w_ref, 2 * turn()))
    a = acc_ref[mine] + by_side(place_pairs(more, sites, count, channels), shape)
    a = a.astype(BF16)
    if first:
        before_ref, done_ref, h_out, *blocks = refs
        whole = jnp.concatenate([before_ref[...], a], axis=0)
    else:
        h_out, a_out, normed_out = refs
        a_out[...] = a
        whole = a
    held = [second_rows(whole, d_ref[...], t_ref, first)]
    held += [rest_ref[row, mine] for row in range(rest_ref.shape[0])]
    weight = reduction(r_ref)
    wide = weight.shape[-1]
    gain = gain_ref[...].astype(F32)
    place = lax.axis_index(AXIS) // group_size
    halves = len(held) // 2
    for half in range(halves):
        left = lanes(
            [held[2 * half + i][:, j].reshape(sites, channels) for i in range(2) for j in range(2)]
        )
        out_row = whole_row(half, halves) if halves > 1 else 0
        residual = dot(left, weight).astype(BF16)
        h_out[:, out_row] = residual.reshape(frames, count, wide)
        residual = residual.astype(F32)
        mean_square = jnp.mean(residual * residual, axis=-1, keepdims=True)
        normed = (residual * lax.rsqrt(mean_square + 1e-06) * gain).astype(BF16)
        normed = normed.reshape(frames, count, wide)
        if not first:
            normed_out[:, out_row] = normed
            continue
        ready = [done_ref[frame, out_row] for frame in range(first)]
        ready += [normed[frame] for frame in range(frames)]
        for frame, value in enumerate(ready):
            for step, block in enumerate(blocks):

                @pl.when(place ^ step == frame)
                def _(block=block, value=value, out_row=out_row):
                    at = out_row * count if halves > 1 else 0
                    block[pl.ds(at, count), :] = value


def scored(mapped, sites):
    scores = lax.dot_general(
        mapped, sites, (((1,), (1,)), ((), ())), preferred_element_type=F32
    ) * (1.0 / math.sqrt(mapped.shape[-1]))
    top = jnp.max(scores, axis=-1, keepdims=True)
    weights = jnp.exp(scores - top)
    return top, jnp.sum(weights, axis=-1, keepdims=True), dot(weights.astype(BF16), sites)


def joined(left, right):
    top = jnp.maximum(left[0], right[0])
    one, two = jnp.exp(left[0] - top), jnp.exp(right[0] - top)
    return top, left[1] * one + right[1] * two, left[2] * one + right[2] * two


def maps_kernel(q_ref, k_ref, v_ref, o_ref, score_ref, out_ref):
    score_ref[...] = lax.dot_general(
        q_ref[...], k_ref[...], (((1,), (1,)), ((), ())), preferred_element_type=F32
    ).astype(BF16)
    out_ref[...] = dot(v_ref[...], o_ref[...]).astype(BF16)


def query_kernel(own_ref, map_ref, out_ref):
    out_ref[...] = dot(own_ref[...], map_ref[...]).astype(BF16)


def early_kernel(mapped_ref, *refs):
    site_refs, outs = refs[:-3], refs[-3:]
    keep(scored(mapped_ref[...], sites_of(site_refs)), *outs)


def keep(stats, top_ref, total_ref, mixed_ref):
    top, total, mixed_ref[...] = stats
    top_ref[...] = jnp.broadcast_to(top, top_ref.shape)
    total_ref[...] = jnp.broadcast_to(total, total_ref.shape)


def sites_of(refs):
    return refs[0][...] if len(refs) == 1 else jnp.concatenate([ref[...] for ref in refs], axis=0)


def next_kernel(mapped_ref, top_ref, total_ref, mixed_ref, *refs):
    site_refs, outs = refs[:-3], refs[-3:]
    held = top_ref[:, :1], total_ref[:, :1], mixed_ref[...]
    keep(joined(held, scored(mapped_ref[...], sites_of(site_refs))), *outs)


def late_kernel(mapped_ref, top_ref, total_ref, mixed_ref, map_ref, *refs, first, parts):
    site_refs, blocks = refs[:parts], refs[parts:]
    count = blocks[0].shape[0]
    mine = slice(first * count, (first + len(blocks)) * count)
    held = top_ref[mine, :1], total_ref[mine, :1], mixed_ref[mine]
    _, total, mixed = joined(held, scored(mapped_ref[mine], sites_of(site_refs)))
    result = dot((mixed / total).astype(BF16), map_ref[...]).astype(BF16)
    for step, block in enumerate(blocks):
        block[...] = result[step * count : (step + 1) * count]


def sum_kernel(a_ref, b_ref, *refs, group_size):
    *blocks, out_ref = refs
    first, rows, count, channels = a_ref.shape
    place = lax.axis_index(AXIS) // group_size
    for step, block in enumerate(blocks):
        value = block[...].astype(F32).reshape(rows, count, channels)
        frame = place ^ step

        @pl.when(frame < first)
        def _(value=value, frame=frame):
            out_ref[frame] = (a_ref[frame].astype(F32) + value).astype(BF16)

        @pl.when(frame >= first)
        def _(value=value, frame=frame):
            out_ref[frame] = (b_ref[frame - first].astype(F32) + value).astype(BF16)


def call(kernel, outs, scratch, args, flops, spaces=None, sems=(), limit=None):
    vmem = pl.BlockSpec(memory_space=pltpu.VMEM)
    shapes = [jax.ShapeDtypeStruct(shape, dtype) for shape, dtype in outs]
    moved = sum(math.prod(arg.shape) * arg.dtype.itemsize for arg in args)
    moved += sum(math.prod(shape) * jnp.dtype(dtype).itemsize for shape, dtype in outs)
    return pl.pallas_call(
        kernel,
        out_shape=shapes,
        in_specs=[pl.BlockSpec(memory_space=space) for space in spaces or [pltpu.VMEM] * len(args)],
        out_specs=[vmem] * len(outs),
        scratch_shapes=[pltpu.VMEM(shape, dtype) for shape, dtype in scratch] + list(sems),
        compiler_params=pltpu.CompilerParams(vmem_limit_bytes=limit or LIMIT),
        cost_estimate=pl.CostEstimate(flops=int(flops), bytes_accessed=int(moved), transcendentals=0),
    )(*args)


LIMIT = 40 * 1024 * 1024


def per_device(
    video,
    s1_weight,
    t1_weight,
    r1_weight,
    s2_weight,
    t2_weight,
    r2_weight,
    attn_gain,
    w_query,
    w_key,
    w_value,
    w_out,
):
    frames, rows, cols, c0 = video.shape
    c1, c2, c3 = s1_weight.shape[-1], s2_weight.shape[-1], w_out.shape[-1]
    count = cols // PHASES
    devices = lax.axis_size(AXIS)
    group_size = devices // frames
    inner = [(d, d ^ 1) for d in range(devices)]
    groups = lax.axis_size("groups")
    outer = [(d, d + 1) for d in range(1, devices - 1, 2)]
    outer = outer + [(target, source) for source, target in outer]
    outer = [(g * devices + a, g * devices + b) for g in range(groups) for a, b in outer]
    if groups % 2 == 0:
        outer += [
            (g * devices + end, (g ^ 1) * devices + end)
            for g in range(groups)
            for end in (0, devices - 1)
        ]
    turns = [
        [(d, (d // group_size ^ k) * group_size + d % group_size) for d in range(devices)]
        for k in range(frames)
    ]

    edge = ((frames, PHASES, count, c1), BF16)
    taps = ((3, frames, cols, c1), F32)
    dma = pltpu.SemaphoreType.DMA
    site_flops = 2 * frames * cols * 3 * c0 * c1
    held = [pltpu.with_memory_space_constraint(x, pltpu.VMEM) for x in (video, s1_weight)]
    video = pltpu.with_memory_space_constraint(video, pltpu.HBM)
    s1_weight = pltpu.with_memory_space_constraint(s1_weight, pltpu.HBM)
    hbm = pltpu.HBM
    part = frames // 2

    (far_a,) = call(
        first_edge_kernel,
        [((part, *edge[0][1:]), BF16)],
        [((part, cols, c0), BF16), ((3, c0, c1), BF16), taps],
        [video, s1_weight],
        site_flops // 2,
        [hbm] * 2,
        [dma((part,)), dma((3,))],
    )
    far_a = lax.ppermute(far_a, BOTH, outer)
    later = frames - part
    far_b, near = call(
        rest_edge_kernel, [((later, *edge[0][1:]), BF16), edge], [taps], held, site_flops * 1.5
    )
    far_b = lax.ppermute(far_b, BOTH, outer)
    near = lax.ppermute(near, AXIS, inner)
    acc, h_next = call(
        front_kernel, [(edge[0], F32), edge], [edge, taps], [*held, t1_weight], 5 * site_flops
    )
    half = (frames, 2, count, c2)
    d_a, a_one = call(
        functools.partial(far_kernel, first=0),
        [((part, *half[1:]), BF16), ((part, *edge[0][1:]), BF16)],
        [],
        [acc, far_a, h_next, t1_weight, r1_weight],
        1e8,
    )
    far_two = lax.ppermute(d_a, BOTH, outer)
    rest = ((rows // 2 - 1, *half), BF16)
    left_rows = ((rows - 2, *edge[0]), BF16)
    (rest_of,) = call(
        back_rows_kernel,
        [rest],
        [left_rows, left_rows, taps],
        [*held, near, t1_weight, r1_weight],
        9e8,
    )
    near = lax.ppermute(rest_of[-1], AXIS, inner)
    (d_b,) = call(
        functools.partial(far_kernel, first=part),
        [((later, *half[1:]), BF16)],
        [],
        [acc, far_b, h_next, t1_weight, r1_weight, a_one],
        1e8,
    )
    far_two_b = lax.ppermute(d_b, BOTH, outer)
    acc, h_rest = call(
        middle_kernel, [(half, F32), rest], [], [d_a, d_b, rest_of, near, s2_weight, t2_weight], 9e8
    )
    site_rows = rows // 4
    block = ((site_rows * count, c3), BF16)
    gain = attn_gain.reshape(1, c3)
    site = ((part, site_rows, count, c3), BF16)
    residual_a, a_two, normed = call(
        functools.partial(second_kernel, first=0, group_size=group_size),
        [site, ((part, *half[1:]), BF16), site],
        [],
        [acc, far_two, d_a, h_rest, s2_weight, t2_weight, r2_weight, gain],
        3e8,
    )
    residual_b, *blocks = call(
        functools.partial(second_kernel, first=part, group_size=group_size),
        [((later, *site[0][1:]), BF16)] + [block] * frames,
        [],
        [acc, far_two_b, d_b, h_rest, s2_weight, t2_weight, r2_weight, gain, a_two, normed],
        3e8,
    )

    def swap(x, bit):
        return lax.ppermute(x, AXIS, [(d, d ^ bit) for d in range(devices)])

    def join(parts):
        return parts[0] if len(parts) == 1 else jnp.concatenate(parts, axis=0)

    held_blocks = [blocks[0]] + [lax.ppermute(blocks[k], AXIS, turns[k]) for k in range(1, frames)]
    order = (0, *Z_ORDER)
    own = join([held_blocks[k] for k in order])
    bit = group_size // 2
    first_far = [swap(held_blocks[k], bit) for k in Y_ORDER]
    if bit == 2:
        near_parts, last_parts = first_far[:-1], [first_far[-1]]
        last_parts.append(swap(held_blocks[Y_ORDER[-1]], bit + 1))
    else:
        near_parts, last_parts = [join(first_far)], []
        bit //= 2
        while bit > 1:
            near_parts.append(swap(join([own] + near_parts), bit))
            bit //= 2
    weight = ((c3, c3), BF16)
    score_map, out_map = call(
        maps_kernel, [weight, weight], [], [w_query, w_key, w_value, w_out], 5e8
    )
    partner = swap(own, 1)
    (mapped,) = call(query_kernel, [(own.shape, BF16)], [], [own, score_map], 1e8)
    stats = ((own.shape[0], 128), F32)
    sums = [stats, stats, (own.shape, F32)]
    early = call(early_kernel, sums, [], [mapped, own, partner], 3e8)
    near_parts, early = lax.optimization_barrier((near_parts, early))
    far_sites = join(near_parts)
    last_parts.append(swap(far_sites, 1))
    held_sums = call(next_kernel, sums, [], [mapped, *early, far_sites], 2e8)

    def late_blocks(first, after):
        return call(
            functools.partial(late_kernel, first=first, parts=len(last_parts)),
            [block] * (after - first),
            [],
            [mapped, *held_sums, out_map, *last_parts],
            3e8,
        )

    done = dict(zip(order, late_blocks(0, frames)))
    blocks = [done[0]] + [lax.ppermute(done[k], AXIS, turns[k]) for k in range(1, frames)]
    (encoded,) = call(
        functools.partial(sum_kernel, group_size=group_size),
        [((frames, site_rows, count, c3), BF16)],
        [],
        [residual_a, residual_b, *blocks],
        1e6,
    )
    return encoded


def solution(mesh):
    placed = (P("groups", "ha", None, None), P(), P(), P(), P(), P(), P(), P(), P(), P(), P(), P())
    return jax.shard_map(
        per_device,
        mesh=mesh,
        in_specs=placed,
        out_specs=P("groups", "ha", None, None),
        check_vma=False,
    )
```

profile of v0, /device:TPU:0, one launch (start us, length us, event | category | flops | bytes accessed | tf_op | source)
XLA Modules:
  0.0 53.6 jit_solution(3134149036003543270)
XLA Ops:
  0.0 1.4 %copy-done = bf16[4,4,192,192]{3,2,1,0:T(8,128)(2,1)S(1)} copy-done((bf16[4,4,192,192]{3,2,1,0:T(8,128)(2,1)S(1)}, bf16[4,4,192,192]{3,2,1,0:T(8,128)(2,1)}, u32[]{:S(2)}) %copy-start) | copy-done | bytes 1179672
  1.4 1.0 %copy-done.4 = bf16[3,3,192,128]{3,2,1,0:T(8,128)(2,1)S(1)} copy-done((bf16[3,3,192,128]{3,2,1,0:T(8,128)(2,1)S(1)}, bf16[3,3,192,128]{3,2,1,0:T(8,128)(2,1)}, u32[]{:S(2)}) %copy-start.4) | copy-done | bytes 442392
  3.5 1.1 %collective-permute-done.2.near_ref = bf16[4,4,48,128]{3,2,1,0:T(8,128)(2,1)S(1)} collective-permute-done((bf16[4,4,48,128]{3,2,1,0:T(8,128)(2,1)S(1)}, bf16[4,4,48,128]{3,2,1,0:T(8,128)(2,1)S(1)}, u32[]{:S(2)}, u32[]{:S(2)}) %collective-permute-start.2) | collective-permute-done | bytes 196640 | tf_op jit(solution)/shard_map/ppermute | solution.py:539
  4.6 1.7 %shard_map.123.rest_ref = bf16[1,4,2,48,256]{4,3,2,1,0:T(8,128)(2,1)S(1)} custom-call(bf16[4,4,192,192]{3,2,1,0:T(8,128)(2,1)S(1)} %copy-done, bf16[3,3,192,128]{3,2,1,0:T(8,128)(2,1)S(1)} %copy-done.4, bf16[4,4,48,128]{3,2,1,0:T(8,128)(2,1)S(1)} %collective-permute-done.2.near_ref, bf16[3,128,128]{2,1,0:T(8,128)(2,1)S(1)} %copy-done.8, ...), custom_call_target="tpu_custom_call" | custom-call | flops 900000000 | bytes 2375680 | tf_op jit(solution)/shard_map/pallas_call | solution.py:465
  6.7 1.5 %shard_map.119 = bf16[2,4,48,128]{3,2,1,0:T(8,128)(2,1)S(1)} custom-call(bf16[4,4,192,192]{3,2,1,0:T(8,128)(2,1)} %video_ref.7, bf16[3,3,192,128]{3,2,1,0:T(8,128)(2,1)} %w_ref.10), custom_call_target="tpu_custom_call" | custom-call | flops 56623104 | bytes 1720320 | tf_op jit(solution)/shard_map/pallas_call | solution.py:465
  8.2 2.6 %collective-permute-start = (bf16[2,4,48,128]{3,2,1,0:T(8,128)(2,1)S(1)}, bf16[2,4,48,128]{3,2,1,0:T(8,128)(2,1)S(1)}, u32[]{:S(2)}, u32[]{:S(2)}) collective-permute-start(bf16[2,4,48,128]{3,2,1,0:T(8,128)(2,1)S(1)} %shard_map.119), channel_id=1, source_target_pairs={{1,2},{3,4},{5,6},{7,8},{9,10},{11,12},{13,14},{2,1},{4,3},{6,5},{... | collective-permute-start | bytes 294920 | tf_op jit(solution)/shard_map/ppermute | solution.py:533
  10.9 1.3 %shard_map.118 = (f32[4,4,48,128]{3,2,1,0:T(8,128)S(1)}, bf16[4,4,48,128]{3,2,1,0:T(8,128)(2,1)S(1)}) custom-call(bf16[4,4,192,192]{3,2,1,0:T(8,128)(2,1)S(1)} %copy-done.1, bf16[3,3,192,128]{3,2,1,0:T(8,128)(2,1)S(1)} %copy-done.5, bf16[3,128,128]{2,1,0:T(8,128)(2,1)S(1)} %copy-done.8), custom_call_target="tpu_custom_call" | custom-call | flops 566231040 | bytes 2310144 | tf_op jit(solution)/shard_map/pallas_call | solution.py:465
  12.2 1.2 %collective-permute-done.far_ref = bf16[2,4,48,128]{3,2,1,0:T(8,128)(2,1)S(1)} collective-permute-done((bf16[2,4,48,128]{3,2,1,0:T(8,128)(2,1)S(1)}, bf16[2,4,48,128]{3,2,1,0:T(8,128)(2,1)S(1)}, u32[]{:S(2)}, u32[]{:S(2)}) %collective-permute-start) | collective-permute-done | bytes 98336 | tf_op jit(solution)/shard_map/ppermute | solution.py:533
  13.8 2.1 %collective-permute-start.4 = (bf16[2,2,48,256]{3,2,1,0:T(8,128)(2,1)S(1)}, bf16[2,2,48,256]{3,2,1,0:T(8,128)(2,1)S(1)}, u32[]{:S(2)}, u32[]{:S(2)}) collective-permute-start(bf16[2,2,48,256]{3,2,1,0:T(8,128)(2,1)S(1)} %get-tuple-element.41.far_a_ref.d_ref), channel_id=1, source_target_pairs={{1,2},{3,4},{5,6},{7,8},{9,10},{11,12},{13,14},{2,1},{4,3},{6,5},{... | collective-permute-start | bytes 294920 | tf_op jit(solution)/shard_map/ppermute | solution.py:551
  16.4 0.7 %collective-permute-start.5 = (bf16[2,2,48,256]{3,2,1,0:T(8,128)(2,1)S(1)}, bf16[2,2,48,256]{3,2,1,0:T(8,128)(2,1)S(1)}, u32[]{:S(2)}, u32[]{:S(2)}) collective-permute-start(bf16[2,2,48,256]{3,2,1,0:T(8,128)(2,1)S(1)} %shard_map.122.far_b_ref.d_ref), channel_id=1, source_target_pairs={{1,2},{3,4},{5,6},{7,8},{9,10},{11,12},{13,14},{2,1},{4,3},{6,5},{... | collective-permute-start | bytes 294920 | tf_op jit(solution)/shard_map/ppermute | solution.py:569
  17.1 1.3 %shard_map.124 = (f32[4,2,48,256]{3,2,1,0:T(8,128)S(1)}, bf16[1,4,2,48,256]{4,3,2,1,0:T(8,128)(2,1)S(1)}) custom-call(bf16[2,2,48,256]{3,2,1,0:T(8,128)(2,1)S(1)} %get-tuple-element.41.far_a_ref.d_ref, bf16[2,2,48,256]{3,2,1,0:T(8,128)(2,1)S(1)} %shard_map.122.far_b_ref.d_ref, bf16[1,4,2,48,256]{4,3,2,1,0:T(8,128)(2,1)S(1)} %shard_map.123.rest_ref, ...), custom_call_target="tpu_custom_call" | custom-call | flops 900000000 | bytes 2752512 | tf_op jit(solution)/shard_map/pallas_call | solution.py:465
  18.5 0.8 %shard_map.125 = (bf16[2,1,48,512]{3,2,1,0:T(8,128)(2,1)S(1)}, bf16[2,2,48,256]{3,2,1,0:T(8,128)(2,1)S(1)}, bf16[2,1,48,512]{3,2,1,0:T(8,128)(2,1)S(1)}) custom-call(f32[4,2,48,256]{3,2,1,0:T(8,128)S(1)} %get-tuple-element.45.acc_ref, bf16[2,2,48,256]{3,2,1,0:T(8,128)(2,1)S(1)} %collective-permute-done.4.far_ref, ...), custom_call_target="tpu_custom_call" | custom-call | flops 300000000 | bytes 3703808 | tf_op jit(solution)/shard_map/pallas_call | solution.py:465
  19.3 1.8 %collective-permute-done.5.far_ref = bf16[2,2,48,256]{3,2,1,0:T(8,128)(2,1)S(1)} collective-permute-done((bf16[2,2,48,256]{3,2,1,0:T(8,128)(2,1)S(1)}, bf16[2,2,48,256]{3,2,1,0:T(8,128)(2,1)S(1)}, u32[]{:S(2)}, u32[]{:S(2)}) %collective-permute-start.5) | collective-permute-done | bytes 98336 | tf_op jit(solution)/shard_map/ppermute | solution.py:569
  21.1 1.0 %shard_map.126 = (bf16[2,1,48,512]{3,2,1,0:T(8,128)(2,1)S(1)}, bf16[48,512]{1,0:T(8,128)(2,1)S(1)}, bf16[48,512]{1,0:T(8,128)(2,1)S(1)}, bf16[48,512]{1,0:T(8,128)(2,1)S(1)}, bf16[48,512]{1,0:T(8,128)(2,1)S(1)}) custom-call(f32[4,2,48,256]{3,2,1,0:T(8,128)S(1)} %get-tuple-element.45.acc_ref, bf16[2,2,48,256]{3,2,1,0:T(8,128)(2,1)S(1)} %collective-permute-done.5.far_ref, ...), custom_call_target="tpu_custom_call" | custom-call | flops 300000000 | bytes 3900416 | tf_op jit(solution)/shard_map/pallas_call | solution.py:465
  22.1 4.5 %collective-permute-start.6 = (bf16[48,512]{1,0:T(8,128)(2,1)S(1)}, bf16[48,512]{1,0:T(8,128)(2,1)S(1)}, u32[]{:S(2)}, u32[]{:S(2)}) collective-permute-start(bf16[48,512]{1,0:T(8,128)(2,1)S(1)} %get-tuple-element.52), channel_id=1, source_target_pairs={{0,12},{1,13},{2,14},{3,15},{4,8},{5,9},{6,10},{7,11},{8,4},{9,5},... | collective-permute-start | bytes 147464 | tf_op jit(solution)/shard_map/ppermute | solution.py:598
  27.2 1.9 %collective-permute-done.6 = bf16[48,512]{1,0:T(8,128)(2,1)S(1)} collective-permute-done((bf16[48,512]{1,0:T(8,128)(2,1)S(1)}, bf16[48,512]{1,0:T(8,128)(2,1)S(1)}, u32[]{:S(2)}, u32[]{:S(2)}) %collective-permute-start.6) | collective-permute-done | bytes 49184 | tf_op jit(solution)/shard_map/ppermute | solution.py:598
  29.1 1.7 %collective-permute-done.7 = bf16[48,512]{1,0:T(8,128)(2,1)S(1)} collective-permute-done((bf16[48,512]{1,0:T(8,128)(2,1)S(1)}, bf16[48,512]{1,0:T(8,128)(2,1)S(1)}, u32[]{:S(2)}, u32[]{:S(2)}) %collective-permute-start.7) | collective-permute-done | bytes 49184 | tf_op jit(solution)/shard_map/ppermute | solution.py:598
  30.8 1.0 %collective-permute-done.8 = bf16[48,512]{1,0:T(8,128)(2,1)S(1)} collective-permute-done((bf16[48,512]{1,0:T(8,128)(2,1)S(1)}, bf16[48,512]{1,0:T(8,128)(2,1)S(1)}, u32[]{:S(2)}, u32[]{:S(2)}) %collective-permute-start.8) | collective-permute-done | bytes 49184 | tf_op jit(solution)/shard_map/ppermute | solution.py:598
  31.9 1.4 %collective-permute-start.9 = (bf16[48,512]{1,0:T(8,128)(2,1)S(1)}, bf16[48,512]{1,0:T(8,128)(2,1)S(1)}, u32[]{:S(2)}, u32[]{:S(2)}) collective-permute-start(bf16[48,512]{1,0:T(8,128)(2,1)S(1)} %get-tuple-element.51), channel_id=1, source_target_pairs={{0,2},{1,3},{2,0},{3,1},{4,6},{5,7},{6,4},{7,5},{8,10},{9,11},{10,... | collective-permute-start | bytes 147464 | tf_op jit(solution)/shard_map/ppermute | solution.py:593
  33.3 0.7 %collective-permute-start.10 = (bf16[48,512]{1,0:T(8,128)(2,1)S(1)}, bf16[48,512]{1,0:T(8,128)(2,1)S(1)}, u32[]{:S(2)}, u32[]{:S(2)}) collective-permute-start(bf16[48,512]{1,0:T(8,128)(2,1)S(1)} %collective-permute-done.6), channel_id=1, source_target_pairs={{0,2},{1,3},{2,0},{3,1},{4,6},{5,7},{6,4},{7,5},{8,10},{9,11},{10,... | collective-permute-start | bytes 147464 | tf_op jit(solution)/shard_map/ppermute | solution.py:593
  33.9 1.4 %collective-permute-start.11 = (bf16[48,512]{1,0:T(8,128)(2,1)S(1)}, bf16[48,512]{1,0:T(8,128)(2,1)S(1)}, u32[]{:S(2)}, u32[]{:S(2)}) collective-permute-start(bf16[48,512]{1,0:T(8,128)(2,1)S(1)} %collective-permute-done.7), channel_id=1, source_target_pairs={{0,2},{1,3},{2,0},{3,1},{4,6},{5,7},{6,4},{7,5},{8,10},{9,11},{10,... | collective-permute-start | bytes 147464 | tf_op jit(solution)/shard_map/ppermute | solution.py:593
  35.3 0.7 %shard_map.127 = (bf16[512,512]{1,0:T(8,128)(2,1)S(1)}, bf16[512,512]{1,0:T(8,128)(2,1)S(1)}) custom-call(bf16[512,512]{1,0:T(8,128)(2,1)S(1)} %copy-done.9, bf16[512,512]{1,0:T(8,128)(2,1)S(1)} %copy-done.10, bf16[512,512]{1,0:T(8,128)(2,1)S(1)} %copy-done.11, bf16[512,512]{1,0:T(8,128)(2,1)S(1)} %copy-done.12), custom_call_target="tpu_custom_call" | custom-call | flops 500000000 | bytes 3145728 | tf_op jit(solution)/shard_map/pallas_call | solution.py:465
  38.2 1.4 %collective-permute-start.13 = (bf16[48,512]{1,0:T(8,128)(2,1)S(1)}, bf16[48,512]{1,0:T(8,128)(2,1)S(1)}, u32[]{:S(2)}, u32[]{:S(2)}) collective-permute-start(bf16[48,512]{1,0:T(8,128)(2,1)S(1)} %collective-permute-done.8), channel_id=1, source_target_pairs={{0,2},{1,3},{2,0},{3,1},{4,6},{5,7},{6,4},{7,5},{8,10},{9,11},{10,... | collective-permute-start | bytes 147464 | tf_op jit(solution)/shard_map/ppermute | solution.py:593
  40.1 0.8 %shard_map.130 = (f32[192,128]{1,0:T(8,128)S(1)}, f32[192,128]{1,0:T(8,128)S(1)}, f32[192,512]{1,0:T(8,128)S(1)}) custom-call(bf16[192,512]{1,0:T(8,128)(2,1)S(1)} %shard_map.128.mapped_ref, f32[192,128]{1,0:T(8,128)S(1)} %get-tuple-element.59.top_ref, f32[192,128]{1,0:T(8,128)S(1)} %get-tuple-element.60.total_ref, ...), custom_call_target="tpu_custom_call" | custom-call | flops 200000000 | bytes 1523712 | tf_op jit(solution)/shard_map/pallas_call | solution.py:465
  40.9 1.5 %collective-permute-done.13.refs_0_ = bf16[48,512]{1,0:T(8,128)(2,1)S(1)} collective-permute-done((bf16[48,512]{1,0:T(8,128)(2,1)S(1)}, bf16[48,512]{1,0:T(8,128)(2,1)S(1)}, u32[]{:S(2)}, u32[]{:S(2)}) %collective-permute-start.13) | collective-permute-done | bytes 49184 | tf_op jit(solution)/shard_map/ppermute | solution.py:593
  42.4 0.9 %collective-permute-done.14.refs_1_ = bf16[48,512]{1,0:T(8,128)(2,1)S(1)} collective-permute-done((bf16[48,512]{1,0:T(8,128)(2,1)S(1)}, bf16[48,512]{1,0:T(8,128)(2,1)S(1)}, u32[]{:S(2)}, u32[]{:S(2)}) %collective-permute-start.14) | collective-permute-done | bytes 49184 | tf_op jit(solution)/shard_map/ppermute | solution.py:593
  43.4 0.9 %shard_map.131 = (bf16[48,512]{1,0:T(8,128)(2,1)S(1)}, bf16[48,512]{1,0:T(8,128)(2,1)S(1)}, bf16[48,512]{1,0:T(8,128)(2,1)S(1)}, bf16[48,512]{1,0:T(8,128)(2,1)S(1)}) custom-call(bf16[192,512]{1,0:T(8,128)(2,1)S(1)} %shard_map.128.mapped_ref, f32[192,128]{1,0:T(8,128)S(1)} %get-tuple-element.65.top_ref, f32[192,128]{1,0:T(8,128)S(1)} %get-tuple-element.66.total_ref, ...), custom_call_target="tpu_custom_call" | custom-call | flops 300000000 | bytes 1753088 | tf_op jit(solution)/shard_map/pallas_call | solution.py:465
  44.3 1.5 %collective-permute-start.16 = (bf16[48,512]{1,0:T(8,128)(2,1)S(1)}, bf16[48,512]{1,0:T(8,128)(2,1)S(1)}, u32[]{:S(2)}, u32[]{:S(2)}) collective-permute-start(bf16[48,512]{1,0:T(8,128)(2,1)S(1)} %get-tuple-element.70), channel_id=1, source_target_pairs={{0,4},{1,5},{2,6},{3,7},{4,0},{5,1},{6,2},{7,3},{8,12},{9,13},{10,... | collective-permute-start | bytes 147464 | tf_op jit(solution)/shard_map/ppermute | solution.py:636
  45.8 1.0 %collective-permute-start.17 = (bf16[48,512]{1,0:T(8,128)(2,1)S(1)}, bf16[48,512]{1,0:T(8,128)(2,1)S(1)}, u32[]{:S(2)}, u32[]{:S(2)}) collective-permute-start(bf16[48,512]{1,0:T(8,128)(2,1)S(1)} %get-tuple-element.71), channel_id=1, source_target_pairs={{0,8},{1,9},{2,10},{3,11},{4,12},{5,13},{6,14},{7,15},{8,0},{9,1},... | collective-permute-start | bytes 147464 | tf_op jit(solution)/shard_map/ppermute | solution.py:636
  46.8 1.9 %collective-permute-start.18 = (bf16[48,512]{1,0:T(8,128)(2,1)S(1)}, bf16[48,512]{1,0:T(8,128)(2,1)S(1)}, u32[]{:S(2)}, u32[]{:S(2)}) collective-permute-start(bf16[48,512]{1,0:T(8,128)(2,1)S(1)} %get-tuple-element.72), channel_id=1, source_target_pairs={{0,12},{1,13},{2,14},{3,15},{4,8},{5,9},{6,10},{7,11},{8,4},{9,5},... | collective-permute-start | bytes 147464 | tf_op jit(solution)/shard_map/ppermute | solution.py:636
  48.8 4.1 %collective-permute-done.17.refs_2_ = bf16[48,512]{1,0:T(8,128)(2,1)S(1)} collective-permute-done((bf16[48,512]{1,0:T(8,128)(2,1)S(1)}, bf16[48,512]{1,0:T(8,128)(2,1)S(1)}, u32[]{:S(2)}, u32[]{:S(2)}) %collective-permute-start.17) | collective-permute-done | bytes 49184 | tf_op jit(solution)/shard_map/ppermute | solution.py:636
  52.9 0.8 %shard_map.132 = bf16[4,1,48,512]{3,2,1,0:T(8,128)(2,1)} custom-call(bf16[2,1,48,512]{3,2,1,0:T(8,128)(2,1)S(1)} %get-tuple-element.47.a_ref, bf16[2,1,48,512]{3,2,1,0:T(8,128)(2,1)S(1)} %get-tuple-element.50.b_ref, bf16[48,512]{1,0:T(8,128)(2,1)S(1)} %get-tuple-element.69.refs_0_, bf16[48,512]{1,0:T(8,128)(2,1)S(1)} %collective-permute-done.16.refs_1_, ...), custom_call_target="tpu_custom_call" | custom-call | flops 1000000 | bytes 589824 | tf_op jit(solution)/shard_map/pallas_call | solution.py:465
  (57 shorter events, 5.8 us)
Async XLA Ops:
  0.0 1.4 %copy-start = (bf16[4,4,192,192]{3,2,1,0:T(8,128)(2,1)S(1)}, bf16[4,4,192,192]{3,2,1,0:T(8,128)(2,1)}, u32[]{:S(2)}) copy-start(bf16[4,4,192,192]{3,2,1,0:T(8,128)(2,1)} %video_ref.7) | copy-start | bytes 3538948
  2.4 2.2 %copy-start.7 = (bf16[2,2,128,256]{3,2,1,0:T(8,128)(2,1)S(1)}, bf16[2,2,128,256]{3,2,1,0:T(8,128)(2,1)}, u32[]{:S(2)}) copy-start(bf16[2,2,128,256]{3,2,1,0:T(8,128)(2,1)} %r_ref.7) | copy-start | bytes 786436
  2.4 2.2 %copy-start.8 = (bf16[3,128,128]{2,1,0:T(8,128)(2,1)S(1)}, bf16[3,128,128]{2,1,0:T(8,128)(2,1)}, u32[]{:S(2)}) copy-start(bf16[3,128,128]{2,1,0:T(8,128)(2,1)} %t_ref.10) | copy-start | bytes 294916
  3.0 1.6 %collective-permute-start.2 = (bf16[4,4,48,128]{3,2,1,0:T(8,128)(2,1)S(1)}, bf16[4,4,48,128]{3,2,1,0:T(8,128)(2,1)S(1)}, u32[]{:S(2)}, u32[]{:S(2)}) collective-permute-start(bf16[4,4,48,128]{3,2,1,0:T(8,128)(2,1)S(1)} %get-tuple-element.44), channel_id=1, source_target_pairs={{0,1},{1,0},{2,3},{3,2},{4,5},{5,4},{6,7},{7,6},{8,9},{9,8},{10,11... | collective-permute-start | bytes 589832 | tf_op jit(solution)/shard_map/ppermute | solution.py:539
  6.2 4.7 %copy-start.1 = (bf16[4,4,192,192]{3,2,1,0:T(8,128)(2,1)S(1)}, bf16[4,4,192,192]{3,2,1,0:T(8,128)(2,1)}, u32[]{:S(2)}) copy-start(bf16[4,4,192,192]{3,2,1,0:T(8,128)(2,1)} %video_ref.7) | copy-start | bytes 3538948
  6.3 4.7 %copy-start.5 = (bf16[3,3,192,128]{3,2,1,0:T(8,128)(2,1)S(1)}, bf16[3,3,192,128]{3,2,1,0:T(8,128)(2,1)}, u32[]{:S(2)}) copy-start(bf16[3,3,192,128]{3,2,1,0:T(8,128)(2,1)} %w_ref.10) | copy-start | bytes 1327108
  6.3 10.8 %collective-permute-start.3 = (bf16[4,2,48,256]{3,2,1,0:T(8,128)(2,1)S(1)}, bf16[4,2,48,256]{3,2,1,0:T(8,128)(2,1)S(1)}, u32[]{:S(2)}, u32[]{:S(2)}) collective-permute-start(bf16[4,2,48,256]{3,2,1,0:T(8,128)(2,1)S(1)} %bitcast.1), channel_id=1, source_target_pairs={{0,1},{1,0},{2,3},{3,2},{4,5},{5,4},{6,7},{7,6},{8,9},{9,8},{10,11... | collective-permute-start | bytes 589832 | tf_op jit(solution)/shard_map/ppermute | solution.py:561
  8.2 5.2 %collective-permute-start = (bf16[2,4,48,128]{3,2,1,0:T(8,128)(2,1)S(1)}, bf16[2,4,48,128]{3,2,1,0:T(8,128)(2,1)S(1)}, u32[]{:S(2)}, u32[]{:S(2)}) collective-permute-start(bf16[2,4,48,128]{3,2,1,0:T(8,128)(2,1)S(1)} %shard_map.119), channel_id=1, source_target_pairs={{1,2},{3,4},{5,6},{7,8},{9,10},{11,12},{13,14},{2,1},{4,3},{6,5},{... | collective-permute-start | bytes 294920 | tf_op jit(solution)/shard_map/ppermute | solution.py:533
  10.8 5.0 %copy-start.13 = (bf16[512]{0:T(512)(128)(2,1)S(1)}, bf16[512]{0:T(512)(128)(2,1)}, u32[]{:S(2)}) copy-start(bf16[512]{0:T(512)(128)(2,1)} %param.19) | copy-start | bytes 3076
  10.8 5.0 %collective-permute-start.1 = (bf16[2,4,48,128]{3,2,1,0:T(8,128)(2,1)S(1)}, bf16[2,4,48,128]{3,2,1,0:T(8,128)(2,1)S(1)}, u32[]{:S(2)}, u32[]{:S(2)}) collective-permute-start(bf16[2,4,48,128]{3,2,1,0:T(8,128)(2,1)S(1)} %get-tuple-element.42), channel_id=1, source_target_pairs={{1,2},{3,4},{5,6},{7,8},{9,10},{11,12},{13,14},{2,1},{4,3},{6,5},{... | collective-permute-start | bytes 294920 | tf_op jit(solution)/shard_map/ppermute | solution.py:538
  12.2 4.9 %copy-start.2 = (bf16[3,3,256,256]{3,2,1,0:T(8,128)(2,1)S(1)}, bf16[3,3,256,256]{3,2,1,0:T(8,128)(2,1)}, u32[]{:S(2)}) copy-start(bf16[3,3,256,256]{3,2,1,0:T(8,128)(2,1)} %w_ref.13) | copy-start | bytes 3538948
  12.2 4.9 %copy-start.6 = (bf16[3,256,256]{2,1,0:T(8,128)(2,1)S(1)}, bf16[3,256,256]{2,1,0:T(8,128)(2,1)}, u32[]{:S(2)}) copy-start(bf16[3,256,256]{2,1,0:T(8,128)(2,1)} %t_ref.13) | copy-start | bytes 1179652
  13.8 4.7 %collective-permute-start.4 = (bf16[2,2,48,256]{3,2,1,0:T(8,128)(2,1)S(1)}, bf16[2,2,48,256]{3,2,1,0:T(8,128)(2,1)S(1)}, u32[]{:S(2)}, u32[]{:S(2)}) collective-permute-start(bf16[2,2,48,256]{3,2,1,0:T(8,128)(2,1)S(1)} %get-tuple-element.41.far_a_ref.d_ref), channel_id=1, source_target_pairs={{1,2},{3,4},{5,6},{7,8},{9,10},{11,12},{13,14},{2,1},{4,3},{6,5},{... | collective-permute-start | bytes 294920 | tf_op jit(solution)/shard_map/ppermute | solution.py:551
  16.4 2.1 %copy-start.3 = (bf16[2,2,256,512]{3,2,1,0:T(8,128)(2,1)S(1)}, bf16[2,2,256,512]{3,2,1,0:T(8,128)(2,1)}, u32[]{:S(2)}) copy-start(bf16[2,2,256,512]{3,2,1,0:T(8,128)(2,1)} %r_ref.9) | copy-start | bytes 3145732
  16.4 4.7 %collective-permute-start.5 = (bf16[2,2,48,256]{3,2,1,0:T(8,128)(2,1)S(1)}, bf16[2,2,48,256]{3,2,1,0:T(8,128)(2,1)S(1)}, u32[]{:S(2)}, u32[]{:S(2)}) collective-permute-start(bf16[2,2,48,256]{3,2,1,0:T(8,128)(2,1)S(1)} %shard_map.122.far_b_ref.d_ref), channel_id=1, source_target_pairs={{1,2},{3,4},{5,6},{7,8},{9,10},{11,12},{13,14},{2,1},{4,3},{6,5},{... | collective-permute-start | bytes 294920 | tf_op jit(solution)/shard_map/ppermute | solution.py:569
  21.1 14.2 %copy-start.9 = (bf16[512,512]{1,0:T(8,128)(2,1)S(1)}, bf16[512,512]{1,0:T(8,128)(2,1)}, u32[]{:S(2)}) copy-start(bf16[512,512]{1,0:T(8,128)(2,1)} %q_ref.1) | copy-start | bytes 1572868
  21.1 14.2 %copy-start.10 = (bf16[512,512]{1,0:T(8,128)(2,1)S(1)}, bf16[512,512]{1,0:T(8,128)(2,1)}, u32[]{:S(2)}) copy-start(bf16[512,512]{1,0:T(8,128)(2,1)} %k_ref.1) | copy-start | bytes 1572868
  21.1 14.2 %copy-start.11 = (bf16[512,512]{1,0:T(8,128)(2,1)S(1)}, bf16[512,512]{1,0:T(8,128)(2,1)}, u32[]{:S(2)}) copy-start(bf16[512,512]{1,0:T(8,128)(2,1)} %v_ref.1) | copy-start | bytes 1572868
  21.1 14.2 %copy-start.12 = (bf16[512,512]{1,0:T(8,128)(2,1)S(1)}, bf16[512,512]{1,0:T(8,128)(2,1)}, u32[]{:S(2)}) copy-start(bf16[512,512]{1,0:T(8,128)(2,1)} %o_ref.1) | copy-start | bytes 1572868
  22.1 7.0 %collective-permute-start.6 = (bf16[48,512]{1,0:T(8,128)(2,1)S(1)}, bf16[48,512]{1,0:T(8,128)(2,1)S(1)}, u32[]{:S(2)}, u32[]{:S(2)}) collective-permute-start(bf16[48,512]{1,0:T(8,128)(2,1)S(1)} %get-tuple-element.52), channel_id=1, source_target_pairs={{0,12},{1,13},{2,14},{3,15},{4,8},{5,9},{6,10},{7,11},{8,4},{9,5},... | collective-permute-start | bytes 147464 | tf_op jit(solution)/shard_map/ppermute | solution.py:598
  26.6 4.2 %collective-permute-start.7 = (bf16[48,512]{1,0:T(8,128)(2,1)S(1)}, bf16[48,512]{1,0:T(8,128)(2,1)S(1)}, u32[]{:S(2)}, u32[]{:S(2)}) collective-permute-start(bf16[48,512]{1,0:T(8,128)(2,1)S(1)} %get-tuple-element.53), channel_id=1, source_target_pairs={{0,4},{1,5},{2,6},{3,7},{4,0},{5,1},{6,2},{7,3},{8,12},{9,13},{10,... | collective-permute-start | bytes 147464 | tf_op jit(solution)/shard_map/ppermute | solution.py:598
  26.6 5.3 %collective-permute-start.8 = (bf16[48,512]{1,0:T(8,128)(2,1)S(1)}, bf16[48,512]{1,0:T(8,128)(2,1)S(1)}, u32[]{:S(2)}, u32[]{:S(2)}) collective-permute-start(bf16[48,512]{1,0:T(8,128)(2,1)S(1)} %get-tuple-element.54), channel_id=1, source_target_pairs={{0,8},{1,9},{2,10},{3,11},{4,12},{5,13},{6,14},{7,15},{8,0},{9,1},... | collective-permute-start | bytes 147464 | tf_op jit(solution)/shard_map/ppermute | solution.py:598
  31.8 4.5 %collective-permute-start.12 = (bf16[192,512]{1,0:T(8,128)(2,1)S(1)}, bf16[192,512]{1,0:T(8,128)(2,1)S(1)}, u32[]{:S(2)}, u32[]{:S(2)}) collective-permute-start(bf16[192,512]{1,0:T(8,128)(2,1)S(1)} %constant_dynamic-update-slice_fusion.own_ref.refs_0_), channel_id=1, source_target_pairs={{0,1},{1,0},{2,3},{3,2},{4,5},{5,4},{6,7},{7,6},{8,9},{9,8},{10,11... | collective-permute-start | bytes 589832 | tf_op jit(solution)/shard_map/ppermute | solution.py:593
  31.9 5.1 %collective-permute-start.9 = (bf16[48,512]{1,0:T(8,128)(2,1)S(1)}, bf16[48,512]{1,0:T(8,128)(2,1)S(1)}, u32[]{:S(2)}, u32[]{:S(2)}) collective-permute-start(bf16[48,512]{1,0:T(8,128)(2,1)S(1)} %get-tuple-element.51), channel_id=1, source_target_pairs={{0,2},{1,3},{2,0},{3,1},{4,6},{5,7},{6,4},{7,5},{8,10},{9,11},{10,... | collective-permute-start | bytes 147464 | tf_op jit(solution)/shard_map/ppermute | solution.py:593
  33.3 4.3 %collective-permute-start.10 = (bf16[48,512]{1,0:T(8,128)(2,1)S(1)}, bf16[48,512]{1,0:T(8,128)(2,1)S(1)}, u32[]{:S(2)}, u32[]{:S(2)}) collective-permute-start(bf16[48,512]{1,0:T(8,128)(2,1)S(1)} %collective-permute-done.6), channel_id=1, source_target_pairs={{0,2},{1,3},{2,0},{3,1},{4,6},{5,7},{6,4},{7,5},{8,10},{9,11},{10,... | collective-permute-start | bytes 147464 | tf_op jit(solution)/shard_map/ppermute | solution.py:593
  33.9 4.2 %collective-permute-start.11 = (bf16[48,512]{1,0:T(8,128)(2,1)S(1)}, bf16[48,512]{1,0:T(8,128)(2,1)S(1)}, u32[]{:S(2)}, u32[]{:S(2)}) collective-permute-start(bf16[48,512]{1,0:T(8,128)(2,1)S(1)} %collective-permute-done.7), channel_id=1, source_target_pairs={{0,2},{1,3},{2,0},{3,1},{4,6},{5,7},{6,4},{7,5},{8,10},{9,11},{10,... | collective-permute-start | bytes 147464 | tf_op jit(solution)/shard_map/ppermute | solution.py:593
  38.2 5.2 %collective-permute-start.15 = (bf16[144,512]{1,0:T(8,128)(2,1)S(1)}, bf16[144,512]{1,0:T(8,128)(2,1)S(1)}, u32[]{:S(2)}, u32[]{:S(2)}) collective-permute-start(bf16[144,512]{1,0:T(8,128)(2,1)S(1)} %constant_dynamic-update-slice_fusion.4.refs_0_), channel_id=1, source_target_pairs={{0,1},{1,0},{2,3},{3,2},{4,5},{5,4},{6,7},{7,6},{8,9},{9,8},{10,11... | collective-permute-start | bytes 442376 | tf_op jit(solution)/shard_map/ppermute | solution.py:593
  38.2 4.2 %collective-permute-start.13 = (bf16[48,512]{1,0:T(8,128)(2,1)S(1)}, bf16[48,512]{1,0:T(8,128)(2,1)S(1)}, u32[]{:S(2)}, u32[]{:S(2)}) collective-permute-start(bf16[48,512]{1,0:T(8,128)(2,1)S(1)} %collective-permute-done.8), channel_id=1, source_target_pairs={{0,2},{1,3},{2,0},{3,1},{4,6},{5,7},{6,4},{7,5},{8,10},{9,11},{10,... | collective-permute-start | bytes 147464 | tf_op jit(solution)/shard_map/ppermute | solution.py:593
  39.6 3.7 %collective-permute-start.14 = (bf16[48,512]{1,0:T(8,128)(2,1)S(1)}, bf16[48,512]{1,0:T(8,128)(2,1)S(1)}, u32[]{:S(2)}, u32[]{:S(2)}) collective-permute-start(bf16[48,512]{1,0:T(8,128)(2,1)S(1)} %collective-permute-done.8), channel_id=1, source_target_pairs={{0,3},{1,2},{2,1},{3,0},{4,7},{5,6},{6,5},{7,4},{8,11},{9,10},{10,... | collective-permute-start | bytes 147464 | tf_op jit(solution)/shard_map/ppermute | solution.py:593
  44.3 4.5 %collective-permute-start.16 = (bf16[48,512]{1,0:T(8,128)(2,1)S(1)}, bf16[48,512]{1,0:T(8,128)(2,1)S(1)}, u32[]{:S(2)}, u32[]{:S(2)}) collective-permute-start(bf16[48,512]{1,0:T(8,128)(2,1)S(1)} %get-tuple-element.70), channel_id=1, source_target_pairs={{0,4},{1,5},{2,6},{3,7},{4,0},{5,1},{6,2},{7,3},{8,12},{9,13},{10,... | collective-permute-start | bytes 147464 | tf_op jit(solution)/shard_map/ppermute | solution.py:636
  45.8 7.1 %collective-permute-start.17 = (bf16[48,512]{1,0:T(8,128)(2,1)S(1)}, bf16[48,512]{1,0:T(8,128)(2,1)S(1)}, u32[]{:S(2)}, u32[]{:S(2)}) collective-permute-start(bf16[48,512]{1,0:T(8,128)(2,1)S(1)} %get-tuple-element.71), channel_id=1, source_target_pairs={{0,8},{1,9},{2,10},{3,11},{4,12},{5,13},{6,14},{7,15},{8,0},{9,1},... | collective-permute-start | bytes 147464 | tf_op jit(solution)/shard_map/ppermute | solution.py:636
  46.8 6.1 %collective-permute-start.18 = (bf16[48,512]{1,0:T(8,128)(2,1)S(1)}, bf16[48,512]{1,0:T(8,128)(2,1)S(1)}, u32[]{:S(2)}, u32[]{:S(2)}) collective-permute-start(bf16[48,512]{1,0:T(8,128)(2,1)S(1)} %get-tuple-element.72), channel_id=1, source_target_pairs={{0,12},{1,13},{2,14},{3,15},{4,8},{5,9},{6,10},{7,11},{8,4},{9,5},... | collective-permute-start | bytes 147464 | tf_op jit(solution)/shard_map/ppermute | solution.py:636
  (1 other events, 1.0 us)
where the time goes:
time: 53.8 us; the launch traced here: 53.6 us
  starting transfers between devices  21.4 us (40%)
  waiting for transfers between devices  16.4 us (30%)
  Pallas kernels  13.1 us (24%)
  local copies, waits for them, and re-layouts  2.51 us (5%)
    pallas_call x15, Pallas kernels, call(): pl.pallas_call(kernel, out_shape=shapes, in_specs=[pl.BlockSpec(memory_sp...  13.1 us
    ppermute x7, starting transfers between devices, swap(): return lax.ppermute(x, AXIS, [(d, d ^ bit) for d in range(devices)])  5.37 us
    ppermute x3, starting transfers between devices, per_device(): lax.ppermute(blocks[k], AXIS, turns[k])  5.11 us
    ppermute x3, waiting for transfers between devices, per_device(): lax.ppermute(blocks[k], AXIS, turns[k])  4.62 us
    ppermute x3, starting transfers between devices, per_device(): lax.ppermute(done[k], AXIS, turns[k])  4.45 us
    ppermute x3, waiting for transfers between devices, per_device(): lax.ppermute(done[k], AXIS, turns[k])  4.13 us
    ppermute x7, waiting for transfers between devices, swap(): return lax.ppermute(x, AXIS, [(d, d ^ bit) for d in range(devices)])  3.61 us
    ppermute x1, starting transfers between devices, per_device(): far_a = lax.ppermute(far_a, BOTH, outer)  2.64 us
  transfers between devices with their start and end apart: 19, of which 11 were waited for; matrix products, arithmetic and copies ran while one was open for 0% of the time, Pallas kernels for 15%

commit v1 on v0

--- a/solution.py
+++ b/solution.py
@@ -14,10 +14,6 @@
 AXIS = "ha"
 BOTH = ("groups", AXIS)
 PHASES = 4
-
-
-Z_ORDER = (3, 1, 2)
-Y_ORDER = (0, 3, 1, 2)
 
 
 def dot(left, right):
@@ -595,14 +591,14 @@
     def join(parts):
         return parts[0] if len(parts) == 1 else jnp.concatenate(parts, axis=0)
 
-    held_blocks = [blocks[0]] + [lax.ppermute(blocks[k], AXIS, turns[k]) for k in range(1, frames)]
-    order = (0, *Z_ORDER)
-    own = join([held_blocks[k] for k in order])
+    order = (0, frames - 1, *range(1, frames - 1))
+    held_blocks = [blocks[0]] + [lax.ppermute(blocks[k], AXIS, turns[k]) for k in order if k]
+    own = join(held_blocks)
     bit = group_size // 2
-    first_far = [swap(held_blocks[k], bit) for k in Y_ORDER]
+    first_far = [swap(x, bit) for x in held_blocks]
     if bit == 2:
         near_parts, last_parts = first_far[:-1], [first_far[-1]]
-        last_parts.append(swap(held_blocks[Y_ORDER[-1]], bit + 1))
+        last_parts.append(swap(held_blocks[-1], bit + 1))
     else:
         near_parts, last_parts = [join(first_far)], []
         bit //= 2

time: 53.8 us -> 53.8 us (level)
  no operation moved by 1% of the time
where the time goes in v1:
time: 53.8 us; the launch traced here: 53.6 us
  starting transfers between devices  21.4 us (40%)
  waiting for transfers between devices  16.4 us (30%)
  Pallas kernels  13.1 us (24%)
  local copies, waits for them, and re-layouts  2.51 us (5%)
    pallas_call x15, Pallas kernels, call(): pl.pallas_call(kernel, out_shape=shapes, in_specs=[pl.BlockSpec(memory_sp...  13.1 us
    ppermute x7, starting transfers between devices, swap(): return lax.ppermute(x, AXIS, [(d, d ^ bit) for d in range(devices)])  5.37 us
    ppermute x3, starting transfers between devices, per_device(): lax.ppermute(blocks[k], AXIS, turns[k])  5.11 us
    ppermute x3, waiting for transfers between devices, per_device(): lax.ppermute(blocks[k], AXIS, turns[k])  4.62 us
    ppermute x3, starting transfers between devices, per_device(): lax.ppermute(done[k], AXIS, turns[k])  4.45 us
    ppermute x3, waiting for transfers between devices, per_device(): lax.ppermute(done[k], AXIS, turns[k])  4.13 us
    ppermute x7, waiting for transfers between devices, swap(): return lax.ppermute(x, AXIS, [(d, d ^ bit) for d in range(devices)])  3.61 us
    ppermute x1, starting transfers between devices, per_device(): far_a = lax.ppermute(far_a, BOTH, outer)  2.64 us
  transfers between devices with their start and end apart: 19, of which 11 were waited for; matrix products, arithmetic and copies ran while one was open for 0% of the time, Pallas kernels for 15%

profile of v1, /device:TPU:0, one launch (start us, length us, event | category | flops | bytes accessed | tf_op | source)
XLA Modules:
  0.0 53.6 jit_solution(3134149036003543270)
XLA Ops:
  0.0 1.4 %copy-done = bf16[4,4,192,192]{3,2,1,0:T(8,128)(2,1)S(1)} copy-done((bf16[4,4,192,192]{3,2,1,0:T(8,128)(2,1)S(1)}, bf16[4,4,192,192]{3,2,1,0:T(8,128)(2,1)}, u32[]{:S(2)}) %copy-start) | copy-done | bytes 1179672
  1.4 1.0 %copy-done.4 = bf16[3,3,192,128]{3,2,1,0:T(8,128)(2,1)S(1)} copy-done((bf16[3,3,192,128]{3,2,1,0:T(8,128)(2,1)S(1)}, bf16[3,3,192,128]{3,2,1,0:T(8,128)(2,1)}, u32[]{:S(2)}) %copy-start.4) | copy-done | bytes 442392
  3.5 1.1 %collective-permute-done.2.near_ref = bf16[4,4,48,128]{3,2,1,0:T(8,128)(2,1)S(1)} collective-permute-done((bf16[4,4,48,128]{3,2,1,0:T(8,128)(2,1)S(1)}, bf16[4,4,48,128]{3,2,1,0:T(8,128)(2,1)S(1)}, u32[]{:S(2)}, u32[]{:S(2)}) %collective-permute-start.2) | collective-permute-done | bytes 196640 | tf_op jit(solution)/shard_map/ppermute | solution.py:535
  4.6 1.7 %shard_map.123.rest_ref = bf16[1,4,2,48,256]{4,3,2,1,0:T(8,128)(2,1)S(1)} custom-call(bf16[4,4,192,192]{3,2,1,0:T(8,128)(2,1)S(1)} %copy-done, bf16[3,3,192,128]{3,2,1,0:T(8,128)(2,1)S(1)} %copy-done.4, bf16[4,4,48,128]{3,2,1,0:T(8,128)(2,1)S(1)} %collective-permute-done.2.near_ref, bf16[3,128,128]{2,1,0:T(8,128)(2,1)S(1)} %copy-done.8, ...), custom_call_target="tpu_custom_call" | custom-call | flops 900000000 | bytes 2375680 | tf_op jit(solution)/shard_map/pallas_call | solution.py:461
  6.7 1.5 %shard_map.119 = bf16[2,4,48,128]{3,2,1,0:T(8,128)(2,1)S(1)} custom-call(bf16[4,4,192,192]{3,2,1,0:T(8,128)(2,1)} %video_ref.7, bf16[3,3,192,128]{3,2,1,0:T(8,128)(2,1)} %w_ref.10), custom_call_target="tpu_custom_call" | custom-call | flops 56623104 | bytes 1720320 | tf_op jit(solution)/shard_map/pallas_call | solution.py:461
  8.2 2.6 %collective-permute-start = (bf16[2,4,48,128]{3,2,1,0:T(8,128)(2,1)S(1)}, bf16[2,4,48,128]{3,2,1,0:T(8,128)(2,1)S(1)}, u32[]{:S(2)}, u32[]{:S(2)}) collective-permute-start(bf16[2,4,48,128]{3,2,1,0:T(8,128)(2,1)S(1)} %shard_map.119), channel_id=1, source_target_pairs={{1,2},{3,4},{5,6},{7,8},{9,10},{11,12},{13,14},{2,1},{4,3},{6,5},{... | collective-permute-start | bytes 294920 | tf_op jit(solution)/shard_map/ppermute | solution.py:529
  10.9 1.3 %shard_map.118 = (f32[4,4,48,128]{3,2,1,0:T(8,128)S(1)}, bf16[4,4,48,128]{3,2,1,0:T(8,128)(2,1)S(1)}) custom-call(bf16[4,4,192,192]{3,2,1,0:T(8,128)(2,1)S(1)} %copy-done.1, bf16[3,3,192,128]{3,2,1,0:T(8,128)(2,1)S(1)} %copy-done.5, bf16[3,128,128]{2,1,0:T(8,128)(2,1)S(1)} %copy-done.8), custom_call_target="tpu_custom_call" | custom-call | flops 566231040 | bytes 2310144 | tf_op jit(solution)/shard_map/pallas_call | solution.py:461
  12.2 1.2 %collective-permute-done.far_ref = bf16[2,4,48,128]{3,2,1,0:T(8,128)(2,1)S(1)} collective-permute-done((bf16[2,4,48,128]{3,2,1,0:T(8,128)(2,1)S(1)}, bf16[2,4,48,128]{3,2,1,0:T(8,128)(2,1)S(1)}, u32[]{:S(2)}, u32[]{:S(2)}) %collective-permute-start) | collective-permute-done | bytes 98336 | tf_op jit(solution)/shard_map/ppermute | solution.py:529
  13.8 2.1 %collective-permute-start.4 = (bf16[2,2,48,256]{3,2,1,0:T(8,128)(2,1)S(1)}, bf16[2,2,48,256]{3,2,1,0:T(8,128)(2,1)S(1)}, u32[]{:S(2)}, u32[]{:S(2)}) collective-permute-start(bf16[2,2,48,256]{3,2,1,0:T(8,128)(2,1)S(1)} %get-tuple-element.41.far_a_ref.d_ref), channel_id=1, source_target_pairs={{1,2},{3,4},{5,6},{7,8},{9,10},{11,12},{13,14},{2,1},{4,3},{6,5},{... | collective-permute-start | bytes 294920 | tf_op jit(solution)/shard_map/ppermute | solution.py:547
  16.4 0.7 %collective-permute-start.5 = (bf16[2,2,48,256]{3,2,1,0:T(8,128)(2,1)S(1)}, bf16[2,2,48,256]{3,2,1,0:T(8,128)(2,1)S(1)}, u32[]{:S(2)}, u32[]{:S(2)}) collective-permute-start(bf16[2,2,48,256]{3,2,1,0:T(8,128)(2,1)S(1)} %shard_map.122.far_b_ref.d_ref), channel_id=1, source_target_pairs={{1,2},{3,4},{5,6},{7,8},{9,10},{11,12},{13,14},{2,1},{4,3},{6,5},{... | collective-permute-start | bytes 294920 | tf_op jit(solution)/shard_map/ppermute | solution.py:565
  17.1 1.3 %shard_map.124 = (f32[4,2,48,256]{3,2,1,0:T(8,128)S(1)}, bf16[1,4,2,48,256]{4,3,2,1,0:T(8,128)(2,1)S(1)}) custom-call(bf16[2,2,48,256]{3,2,1,0:T(8,128)(2,1)S(1)} %get-tuple-element.41.far_a_ref.d_ref, bf16[2,2,48,256]{3,2,1,0:T(8,128)(2,1)S(1)} %shard_map.122.far_b_ref.d_ref, bf16[1,4,2,48,256]{4,3,2,1,0:T(8,128)(2,1)S(1)} %shard_map.123.rest_ref, ...), custom_call_target="tpu_custom_call" | custom-call | flops 900000000 | bytes 2752512 | tf_op jit(solution)/shard_map/pallas_call | solution.py:461
  18.5 0.8 %shard_map.125 = (bf16[2,1,48,512]{3,2,1,0:T(8,128)(2,1)S(1)}, bf16[2,2,48,256]{3,2,1,0:T(8,128)(2,1)S(1)}, bf16[2,1,48,512]{3,2,1,0:T(8,128)(2,1)S(1)}) custom-call(f32[4,2,48,256]{3,2,1,0:T(8,128)S(1)} %get-tuple-element.45.acc_ref, bf16[2,2,48,256]{3,2,1,0:T(8,128)(2,1)S(1)} %collective-permute-done.4.far_ref, ...), custom_call_target="tpu_custom_call" | custom-call | flops 300000000 | bytes 3703808 | tf_op jit(solution)/shard_map/pallas_call | solution.py:461
  19.3 1.8 %collective-permute-done.5.far_ref = bf16[2,2,48,256]{3,2,1,0:T(8,128)(2,1)S(1)} collective-permute-done((bf16[2,2,48,256]{3,2,1,0:T(8,128)(2,1)S(1)}, bf16[2,2,48,256]{3,2,1,0:T(8,128)(2,1)S(1)}, u32[]{:S(2)}, u32[]{:S(2)}) %collective-permute-start.5) | collective-permute-done | bytes 98336 | tf_op jit(solution)/shard_map/ppermute | solution.py:565
  21.1 1.0 %shard_map.126 = (bf16[2,1,48,512]{3,2,1,0:T(8,128)(2,1)S(1)}, bf16[48,512]{1,0:T(8,128)(2,1)S(1)}, bf16[48,512]{1,0:T(8,128)(2,1)S(1)}, bf16[48,512]{1,0:T(8,128)(2,1)S(1)}, bf16[48,512]{1,0:T(8,128)(2,1)S(1)}) custom-call(f32[4,2,48,256]{3,2,1,0:T(8,128)S(1)} %get-tuple-element.45.acc_ref, bf16[2,2,48,256]{3,2,1,0:T(8,128)(2,1)S(1)} %collective-permute-done.5.far_ref, ...), custom_call_target="tpu_custom_call" | custom-call | flops 300000000 | bytes 3900416 | tf_op jit(solution)/shard_map/pallas_call | solution.py:461
  22.1 4.5 %collective-permute-start.6 = (bf16[48,512]{1,0:T(8,128)(2,1)S(1)}, bf16[48,512]{1,0:T(8,128)(2,1)S(1)}, u32[]{:S(2)}, u32[]{:S(2)}) collective-permute-start(bf16[48,512]{1,0:T(8,128)(2,1)S(1)} %get-tuple-element.52), channel_id=1, source_target_pairs={{0,12},{1,13},{2,14},{3,15},{4,8},{5,9},{6,10},{7,11},{8,4},{9,5},... | collective-permute-start | bytes 147464 | tf_op jit(solution)/shard_map/ppermute | solution.py:595
  27.2 1.9 %collective-permute-done.6 = bf16[48,512]{1,0:T(8,128)(2,1)S(1)} collective-permute-done((bf16[48,512]{1,0:T(8,128)(2,1)S(1)}, bf16[48,512]{1,0:T(8,128)(2,1)S(1)}, u32[]{:S(2)}, u32[]{:S(2)}) %collective-permute-start.6) | collective-permute-done | bytes 49184 | tf_op jit(solution)/shard_map/ppermute | solution.py:595
  29.1 1.7 %collective-permute-done.7 = bf16[48,512]{1,0:T(8,128)(2,1)S(1)} collective-permute-done((bf16[48,512]{1,0:T(8,128)(2,1)S(1)}, bf16[48,512]{1,0:T(8,128)(2,1)S(1)}, u32[]{:S(2)}, u32[]{:S(2)}) %collective-permute-start.7) | collective-permute-done | bytes 49184 | tf_op jit(solution)/shard_map/ppermute | solution.py:595
  30.8 1.0 %collective-permute-done.8 = bf16[48,512]{1,0:T(8,128)(2,1)S(1)} collective-permute-done((bf16[48,512]{1,0:T(8,128)(2,1)S(1)}, bf16[48,512]{1,0:T(8,128)(2,1)S(1)}, u32[]{:S(2)}, u32[]{:S(2)}) %collective-permute-start.8) | collective-permute-done | bytes 49184 | tf_op jit(solution)/shard_map/ppermute | solution.py:595
  31.9 1.4 %collective-permute-start.9 = (bf16[48,512]{1,0:T(8,128)(2,1)S(1)}, bf16[48,512]{1,0:T(8,128)(2,1)S(1)}, u32[]{:S(2)}, u32[]{:S(2)}) collective-permute-start(bf16[48,512]{1,0:T(8,128)(2,1)S(1)} %get-tuple-element.51), channel_id=1, source_target_pairs={{0,2},{1,3},{2,0},{3,1},{4,6},{5,7},{6,4},{7,5},{8,10},{9,11},{10,... | collective-permute-start | bytes 147464 | tf_op jit(solution)/shard_map/ppermute | solution.py:589
  33.3 0.7 %collective-permute-start.10 = (bf16[48,512]{1,0:T(8,128)(2,1)S(1)}, bf16[48,512]{1,0:T(8,128)(2,1)S(1)}, u32[]{:S(2)}, u32[]{:S(2)}) collective-permute-start(bf16[48,512]{1,0:T(8,128)(2,1)S(1)} %collective-permute-done.6), channel_id=1, source_target_pairs={{0,2},{1,3},{2,0},{3,1},{4,6},{5,7},{6,4},{7,5},{8,10},{9,11},{10,... | collective-permute-start | bytes 147464 | tf_op jit(solution)/shard_map/ppermute | solution.py:589
  33.9 1.4 %collective-permute-start.11 = (bf16[48,512]{1,0:T(8,128)(2,1)S(1)}, bf16[48,512]{1,0:T(8,128)(2,1)S(1)}, u32[]{:S(2)}, u32[]{:S(2)}) collective-permute-start(bf16[48,512]{1,0:T(8,128)(2,1)S(1)} %collective-permute-done.7), channel_id=1, source_target_pairs={{0,2},{1,3},{2,0},{3,1},{4,6},{5,7},{6,4},{7,5},{8,10},{9,11},{10,... | collective-permute-start | bytes 147464 | tf_op jit(solution)/shard_map/ppermute | solution.py:589
  35.3 0.7 %shard_map.127 = (bf16[512,512]{1,0:T(8,128)(2,1)S(1)}, bf16[512,512]{1,0:T(8,128)(2,1)S(1)}) custom-call(bf16[512,512]{1,0:T(8,128)(2,1)S(1)} %copy-done.9, bf16[512,512]{1,0:T(8,128)(2,1)S(1)} %copy-done.10, bf16[512,512]{1,0:T(8,128)(2,1)S(1)} %copy-done.11, bf16[512,512]{1,0:T(8,128)(2,1)S(1)} %copy-done.12), custom_call_target="tpu_custom_call" | custom-call | flops 500000000 | bytes 3145728 | tf_op jit(solution)/shard_map/pallas_call | solution.py:461
  38.2 1.4 %collective-permute-start.13 = (bf16[48,512]{1,0:T(8,128)(2,1)S(1)}, bf16[48,512]{1,0:T(8,128)(2,1)S(1)}, u32[]{:S(2)}, u32[]{:S(2)}) collective-permute-start(bf16[48,512]{1,0:T(8,128)(2,1)S(1)} %collective-permute-done.8), channel_id=1, source_target_pairs={{0,2},{1,3},{2,0},{3,1},{4,6},{5,7},{6,4},{7,5},{8,10},{9,11},{10,... | collective-permute-start | bytes 147464 | tf_op jit(solution)/shard_map/ppermute | solution.py:589
  40.1 0.8 %shard_map.130 = (f32[192,128]{1,0:T(8,128)S(1)}, f32[192,128]{1,0:T(8,128)S(1)}, f32[192,512]{1,0:T(8,128)S(1)}) custom-call(bf16[192,512]{1,0:T(8,128)(2,1)S(1)} %shard_map.128.mapped_ref, f32[192,128]{1,0:T(8,128)S(1)} %get-tuple-element.59.top_ref, f32[192,128]{1,0:T(8,128)S(1)} %get-tuple-element.60.total_ref, ...), custom_call_target="tpu_custom_call" | custom-call | flops 200000000 | bytes 1523712 | tf_op jit(solution)/shard_map/pallas_call | solution.py:461
  40.9 1.5 %collective-permute-done.13.refs_0_ = bf16[48,512]{1,0:T(8,128)(2,1)S(1)} collective-permute-done((bf16[48,512]{1,0:T(8,128)(2,1)S(1)}, bf16[48,512]{1,0:T(8,128)(2,1)S(1)}, u32[]{:S(2)}, u32[]{:S(2)}) %collective-permute-start.13) | collective-permute-done | bytes 49184 | tf_op jit(solution)/shard_map/ppermute | solution.py:589
  42.4 0.9 %collective-permute-done.14.refs_1_ = bf16[48,512]{1,0:T(8,128)(2,1)S(1)} collective-permute-done((bf16[48,512]{1,0:T(8,128)(2,1)S(1)}, bf16[48,512]{1,0:T(8,128)(2,1)S(1)}, u32[]{:S(2)}, u32[]{:S(2)}) %collective-permute-start.14) | collective-permute-done | bytes 49184 | tf_op jit(solution)/shard_map/ppermute | solution.py:589
  43.4 0.9 %shard_map.131 = (bf16[48,512]{1,0:T(8,128)(2,1)S(1)}, bf16[48,512]{1,0:T(8,128)(2,1)S(1)}, bf16[48,512]{1,0:T(8,128)(2,1)S(1)}, bf16[48,512]{1,0:T(8,128)(2,1)S(1)}) custom-call(bf16[192,512]{1,0:T(8,128)(2,1)S(1)} %shard_map.128.mapped_ref, f32[192,128]{1,0:T(8,128)S(1)} %get-tuple-element.65.top_ref, f32[192,128]{1,0:T(8,128)S(1)} %get-tuple-element.66.total_ref, ...), custom_call_target="tpu_custom_call" | custom-call | flops 300000000 | bytes 1753088 | tf_op jit(solution)/shard_map/pallas_call | solution.py:461
  44.3 1.5 %collective-permute-start.16 = (bf16[48,512]{1,0:T(8,128)(2,1)S(1)}, bf16[48,512]{1,0:T(8,128)(2,1)S(1)}, u32[]{:S(2)}, u32[]{:S(2)}) collective-permute-start(bf16[48,512]{1,0:T(8,128)(2,1)S(1)} %get-tuple-element.70), channel_id=1, source_target_pairs={{0,4},{1,5},{2,6},{3,7},{4,0},{5,1},{6,2},{7,3},{8,12},{9,13},{10,... | collective-permute-start | bytes 147464 | tf_op jit(solution)/shard_map/ppermute | solution.py:632
  45.8 1.0 %collective-permute-start.17 = (bf16[48,512]{1,0:T(8,128)(2,1)S(1)}, bf16[48,512]{1,0:T(8,128)(2,1)S(1)}, u32[]{:S(2)}, u32[]{:S(2)}) collective-permute-start(bf16[48,512]{1,0:T(8,128)(2,1)S(1)} %get-tuple-element.71), channel_id=1, source_target_pairs={{0,8},{1,9},{2,10},{3,11},{4,12},{5,13},{6,14},{7,15},{8,0},{9,1},... | collective-permute-start | bytes 147464 | tf_op jit(solution)/shard_map/ppermute | solution.py:632
  46.8 1.9 %collective-permute-start.18 = (bf16[48,512]{1,0:T(8,128)(2,1)S(1)}, bf16[48,512]{1,0:T(8,128)(2,1)S(1)}, u32[]{:S(2)}, u32[]{:S(2)}) collective-permute-start(bf16[48,512]{1,0:T(8,128)(2,1)S(1)} %get-tuple-element.72), channel_id=1, source_target_pairs={{0,12},{1,13},{2,14},{3,15},{4,8},{5,9},{6,10},{7,11},{8,4},{9,5},... | collective-permute-start | bytes 147464 | tf_op jit(solution)/shard_map/ppermute | solution.py:632
  48.8 4.1 %collective-permute-done.17.refs_2_ = bf16[48,512]{1,0:T(8,128)(2,1)S(1)} collective-permute-done((bf16[48,512]{1,0:T(8,128)(2,1)S(1)}, bf16[48,512]{1,0:T(8,128)(2,1)S(1)}, u32[]{:S(2)}, u32[]{:S(2)}) %collective-permute-start.17) | collective-permute-done | bytes 49184 | tf_op jit(solution)/shard_map/ppermute | solution.py:632
  52.9 0.8 %shard_map.132 = bf16[4,1,48,512]{3,2,1,0:T(8,128)(2,1)} custom-call(bf16[2,1,48,512]{3,2,1,0:T(8,128)(2,1)S(1)} %get-tuple-element.47.a_ref, bf16[2,1,48,512]{3,2,1,0:T(8,128)(2,1)S(1)} %get-tuple-element.50.b_ref, bf16[48,512]{1,0:T(8,128)(2,1)S(1)} %get-tuple-element.69.refs_0_, bf16[48,512]{1,0:T(8,128)(2,1)S(1)} %collective-permute-done.16.refs_1_, ...), custom_call_target="tpu_custom_call" | custom-call | flops 1000000 | bytes 589824 | tf_op jit(solution)/shard_map/pallas_call | solution.py:461
  (57 shorter events, 5.8 us)
Async XLA Ops:
  0.0 1.4 %copy-start = (bf16[4,4,192,192]{3,2,1,0:T(8,128)(2,1)S(1)}, bf16[4,4,192,192]{3,2,1,0:T(8,128)(2,1)}, u32[]{:S(2)}) copy-start(bf16[4,4,192,192]{3,2,1,0:T(8,128)(2,1)} %video_ref.7) | copy-start | bytes 3538948
  2.4 2.2 %copy-start.7 = (bf16[2,2,128,256]{3,2,1,0:T(8,128)(2,1)S(1)}, bf16[2,2,128,256]{3,2,1,0:T(8,128)(2,1)}, u32[]{:S(2)}) copy-start(bf16[2,2,128,256]{3,2,1,0:T(8,128)(2,1)} %r_ref.7) | copy-start | bytes 786436
  2.4 2.2 %copy-start.8 = (bf16[3,128,128]{2,1,0:T(8,128)(2,1)S(1)}, bf16[3,128,128]{2,1,0:T(8,128)(2,1)}, u32[]{:S(2)}) copy-start(bf16[3,128,128]{2,1,0:T(8,128)(2,1)} %t_ref.10) | copy-start | bytes 294916
  3.0 1.6 %collective-permute-start.2 = (bf16[4,4,48,128]{3,2,1,0:T(8,128)(2,1)S(1)}, bf16[4,4,48,128]{3,2,1,0:T(8,128)(2,1)S(1)}, u32[]{:S(2)}, u32[]{:S(2)}) collective-permute-start(bf16[4,4,48,128]{3,2,1,0:T(8,128)(2,1)S(1)} %get-tuple-element.44), channel_id=1, source_target_pairs={{0,1},{1,0},{2,3},{3,2},{4,5},{5,4},{6,7},{7,6},{8,9},{9,8},{10,11... | collective-permute-start | bytes 589832 | tf_op jit(solution)/shard_map/ppermute | solution.py:535
  6.2 4.7 %copy-start.1 = (bf16[4,4,192,192]{3,2,1,0:T(8,128)(2,1)S(1)}, bf16[4,4,192,192]{3,2,1,0:T(8,128)(2,1)}, u32[]{:S(2)}) copy-start(bf16[4,4,192,192]{3,2,1,0:T(8,128)(2,1)} %video_ref.7) | copy-start | bytes 3538948
  6.3 4.7 %copy-start.5 = (bf16[3,3,192,128]{3,2,1,0:T(8,128)(2,1)S(1)}, bf16[3,3,192,128]{3,2,1,0:T(8,128)(2,1)}, u32[]{:S(2)}) copy-start(bf16[3,3,192,128]{3,2,1,0:T(8,128)(2,1)} %w_ref.10) | copy-start | bytes 1327108
  6.3 10.8 %collective-permute-start.3 = (bf16[4,2,48,256]{3,2,1,0:T(8,128)(2,1)S(1)}, bf16[4,2,48,256]{3,2,1,0:T(8,128)(2,1)S(1)}, u32[]{:S(2)}, u32[]{:S(2)}) collective-permute-start(bf16[4,2,48,256]{3,2,1,0:T(8,128)(2,1)S(1)} %bitcast.1), channel_id=1, source_target_pairs={{0,1},{1,0},{2,3},{3,2},{4,5},{5,4},{6,7},{7,6},{8,9},{9,8},{10,11... | collective-permute-start | bytes 589832 | tf_op jit(solution)/shard_map/ppermute | solution.py:557
  8.2 5.2 %collective-permute-start = (bf16[2,4,48,128]{3,2,1,0:T(8,128)(2,1)S(1)}, bf16[2,4,48,128]{3,2,1,0:T(8,128)(2,1)S(1)}, u32[]{:S(2)}, u32[]{:S(2)}) collective-permute-start(bf16[2,4,48,128]{3,2,1,0:T(8,128)(2,1)S(1)} %shard_map.119), channel_id=1, source_target_pairs={{1,2},{3,4},{5,6},{7,8},{9,10},{11,12},{13,14},{2,1},{4,3},{6,5},{... | collective-permute-start | bytes 294920 | tf_op jit(solution)/shard_map/ppermute | solution.py:529
  10.8 5.0 %copy-start.13 = (bf16[512]{0:T(512)(128)(2,1)S(1)}, bf16[512]{0:T(512)(128)(2,1)}, u32[]{:S(2)}) copy-start(bf16[512]{0:T(512)(128)(2,1)} %param.19) | copy-start | bytes 3076
  10.8 5.0 %collective-permute-start.1 = (bf16[2,4,48,128]{3,2,1,0:T(8,128)(2,1)S(1)}, bf16[2,4,48,128]{3,2,1,0:T(8,128)(2,1)S(1)}, u32[]{:S(2)}, u32[]{:S(2)}) collective-permute-start(bf16[2,4,48,128]{3,2,1,0:T(8,128)(2,1)S(1)} %get-tuple-element.42), channel_id=1, source_target_pairs={{1,2},{3,4},{5,6},{7,8},{9,10},{11,12},{13,14},{2,1},{4,3},{6,5},{... | collective-permute-start | bytes 294920 | tf_op jit(solution)/shard_map/ppermute | solution.py:534
  12.2 4.9 %copy-start.2 = (bf16[3,3,256,256]{3,2,1,0:T(8,128)(2,1)S(1)}, bf16[3,3,256,256]{3,2,1,0:T(8,128)(2,1)}, u32[]{:S(2)}) copy-start(bf16[3,3,256,256]{3,2,1,0:T(8,128)(2,1)} %w_ref.13) | copy-start | bytes 3538948
  12.2 4.9 %copy-start.6 = (bf16[3,256,256]{2,1,0:T(8,128)(2,1)S(1)}, bf16[3,256,256]{2,1,0:T(8,128)(2,1)}, u32[]{:S(2)}) copy-start(bf16[3,256,256]{2,1,0:T(8,128)(2,1)} %t_ref.13) | copy-start | bytes 1179652
  13.8 4.7 %collective-permute-start.4 = (bf16[2,2,48,256]{3,2,1,0:T(8,128)(2,1)S(1)}, bf16[2,2,48,256]{3,2,1,0:T(8,128)(2,1)S(1)}, u32[]{:S(2)}, u32[]{:S(2)}) collective-permute-start(bf16[2,2,48,256]{3,2,1,0:T(8,128)(2,1)S(1)} %get-tuple-element.41.far_a_ref.d_ref), channel_id=1, source_target_pairs={{1,2},{3,4},{5,6},{7,8},{9,10},{11,12},{13,14},{2,1},{4,3},{6,5},{... | collective-permute-start | bytes 294920 | tf_op jit(solution)/shard_map/ppermute | solution.py:547
  16.4 2.1 %copy-start.3 = (bf16[2,2,256,512]{3,2,1,0:T(8,128)(2,1)S(1)}, bf16[2,2,256,512]{3,2,1,0:T(8,128)(2,1)}, u32[]{:S(2)}) copy-start(bf16[2,2,256,512]{3,2,1,0:T(8,128)(2,1)} %r_ref.9) | copy-start | bytes 3145732
  16.4 4.7 %collective-permute-start.5 = (bf16[2,2,48,256]{3,2,1,0:T(8,128)(2,1)S(1)}, bf16[2,2,48,256]{3,2,1,0:T(8,128)(2,1)S(1)}, u32[]{:S(2)}, u32[]{:S(2)}) collective-permute-start(bf16[2,2,48,256]{3,2,1,0:T(8,128)(2,1)S(1)} %shard_map.122.far_b_ref.d_ref), channel_id=1, source_target_pairs={{1,2},{3,4},{5,6},{7,8},{9,10},{11,12},{13,14},{2,1},{4,3},{6,5},{... | collective-permute-start | bytes 294920 | tf_op jit(solution)/shard_map/ppermute | solution.py:565
  21.1 14.2 %copy-start.9 = (bf16[512,512]{1,0:T(8,128)(2,1)S(1)}, bf16[512,512]{1,0:T(8,128)(2,1)}, u32[]{:S(2)}) copy-start(bf16[512,512]{1,0:T(8,128)(2,1)} %q_ref.1) | copy-start | bytes 1572868
  21.1 14.2 %copy-start.10 = (bf16[512,512]{1,0:T(8,128)(2,1)S(1)}, bf16[512,512]{1,0:T(8,128)(2,1)}, u32[]{:S(2)}) copy-start(bf16[512,512]{1,0:T(8,128)(2,1)} %k_ref.1) | copy-start | bytes 1572868
  21.1 14.2 %copy-start.11 = (bf16[512,512]{1,0:T(8,128)(2,1)S(1)}, bf16[512,512]{1,0:T(8,128)(2,1)}, u32[]{:S(2)}) copy-start(bf16[512,512]{1,0:T(8,128)(2,1)} %v_ref.1) | copy-start | bytes 1572868
  21.1 14.2 %copy-start.12 = (bf16[512,512]{1,0:T(8,128)(2,1)S(1)}, bf16[512,512]{1,0:T(8,128)(2,1)}, u32[]{:S(2)}) copy-start(bf16[512,512]{1,0:T(8,128)(2,1)} %o_ref.1) | copy-start | bytes 1572868
  22.1 7.0 %collective-permute-start.6 = (bf16[48,512]{1,0:T(8,128)(2,1)S(1)}, bf16[48,512]{1,0:T(8,128)(2,1)S(1)}, u32[]{:S(2)}, u32[]{:S(2)}) collective-permute-start(bf16[48,512]{1,0:T(8,128)(2,1)S(1)} %get-tuple-element.52), channel_id=1, source_target_pairs={{0,12},{1,13},{2,14},{3,15},{4,8},{5,9},{6,10},{7,11},{8,4},{9,5},... | collective-permute-start | bytes 147464 | tf_op jit(solution)/shard_map/ppermute | solution.py:595
  26.6 4.2 %collective-permute-start.7 = (bf16[48,512]{1,0:T(8,128)(2,1)S(1)}, bf16[48,512]{1,0:T(8,128)(2,1)S(1)}, u32[]{:S(2)}, u32[]{:S(2)}) collective-permute-start(bf16[48,512]{1,0:T(8,128)(2,1)S(1)} %get-tuple-element.53), channel_id=1, source_target_pairs={{0,4},{1,5},{2,6},{3,7},{4,0},{5,1},{6,2},{7,3},{8,12},{9,13},{10,... | collective-permute-start | bytes 147464 | tf_op jit(solution)/shard_map/ppermute | solution.py:595
  26.6 5.3 %collective-permute-start.8 = (bf16[48,512]{1,0:T(8,128)(2,1)S(1)}, bf16[48,512]{1,0:T(8,128)(2,1)S(1)}, u32[]{:S(2)}, u32[]{:S(2)}) collective-permute-start(bf16[48,512]{1,0:T(8,128)(2,1)S(1)} %get-tuple-element.54), channel_id=1, source_target_pairs={{0,8},{1,9},{2,10},{3,11},{4,12},{5,13},{6,14},{7,15},{8,0},{9,1},... | collective-permute-start | bytes 147464 | tf_op jit(solution)/shard_map/ppermute | solution.py:595
  31.8 4.5 %collective-permute-start.12 = (bf16[192,512]{1,0:T(8,128)(2,1)S(1)}, bf16[192,512]{1,0:T(8,128)(2,1)S(1)}, u32[]{:S(2)}, u32[]{:S(2)}) collective-permute-start(bf16[192,512]{1,0:T(8,128)(2,1)S(1)} %constant_dynamic-update-slice_fusion.own_ref.refs_0_), channel_id=1, source_target_pairs={{0,1},{1,0},{2,3},{3,2},{4,5},{5,4},{6,7},{7,6},{8,9},{9,8},{10,11... | collective-permute-start | bytes 589832 | tf_op jit(solution)/shard_map/ppermute | solution.py:589
  31.9 5.1 %collective-permute-start.9 = (bf16[48,512]{1,0:T(8,128)(2,1)S(1)}, bf16[48,512]{1,0:T(8,128)(2,1)S(1)}, u32[]{:S(2)}, u32[]{:S(2)}) collective-permute-start(bf16[48,512]{1,0:T(8,128)(2,1)S(1)} %get-tuple-element.51), channel_id=1, source_target_pairs={{0,2},{1,3},{2,0},{3,1},{4,6},{5,7},{6,4},{7,5},{8,10},{9,11},{10,... | collective-permute-start | bytes 147464 | tf_op jit(solution)/shard_map/ppermute | solution.py:589
  33.3 4.3 %collective-permute-start.10 = (bf16[48,512]{1,0:T(8,128)(2,1)S(1)}, bf16[48,512]{1,0:T(8,128)(2,1)S(1)}, u32[]{:S(2)}, u32[]{:S(2)}) collective-permute-start(bf16[48,512]{1,0:T(8,128)(2,1)S(1)} %collective-permute-done.6), channel_id=1, source_target_pairs={{0,2},{1,3},{2,0},{3,1},{4,6},{5,7},{6,4},{7,5},{8,10},{9,11},{10,... | collective-permute-start | bytes 147464 | tf_op jit(solution)/shard_map/ppermute | solution.py:589
  33.9 4.2 %collective-permute-start.11 = (bf16[48,512]{1,0:T(8,128)(2,1)S(1)}, bf16[48,512]{1,0:T(8,128)(2,1)S(1)}, u32[]{:S(2)}, u32[]{:S(2)}) collective-permute-start(bf16[48,512]{1,0:T(8,128)(2,1)S(1)} %collective-permute-done.7), channel_id=1, source_target_pairs={{0,2},{1,3},{2,0},{3,1},{4,6},{5,7},{6,4},{7,5},{8,10},{9,11},{10,... | collective-permute-start | bytes 147464 | tf_op jit(solution)/shard_map/ppermute | solution.py:589
  38.2 5.2 %collective-permute-start.15 = (bf16[144,512]{1,0:T(8,128)(2,1)S(1)}, bf16[144,512]{1,0:T(8,128)(2,1)S(1)}, u32[]{:S(2)}, u32[]{:S(2)}) collective-permute-start(bf16[144,512]{1,0:T(8,128)(2,1)S(1)} %constant_dynamic-update-slice_fusion.4.refs_0_), channel_id=1, source_target_pairs={{0,1},{1,0},{2,3},{3,2},{4,5},{5,4},{6,7},{7,6},{8,9},{9,8},{10,11... | collective-permute-start | bytes 442376 | tf_op jit(solution)/shard_map/ppermute | solution.py:589
  38.2 4.2 %collective-permute-start.13 = (bf16[48,512]{1,0:T(8,128)(2,1)S(1)}, bf16[48,512]{1,0:T(8,128)(2,1)S(1)}, u32[]{:S(2)}, u32[]{:S(2)}) collective-permute-start(bf16[48,512]{1,0:T(8,128)(2,1)S(1)} %collective-permute-done.8), channel_id=1, source_target_pairs={{0,2},{1,3},{2,0},{3,1},{4,6},{5,7},{6,4},{7,5},{8,10},{9,11},{10,... | collective-permute-start | bytes 147464 | tf_op jit(solution)/shard_map/ppermute | solution.py:589
  39.6 3.7 %collective-permute-start.14 = (bf16[48,512]{1,0:T(8,128)(2,1)S(1)}, bf16[48,512]{1,0:T(8,128)(2,1)S(1)}, u32[]{:S(2)}, u32[]{:S(2)}) collective-permute-start(bf16[48,512]{1,0:T(8,128)(2,1)S(1)} %collective-permute-done.8), channel_id=1, source_target_pairs={{0,3},{1,2},{2,1},{3,0},{4,7},{5,6},{6,5},{7,4},{8,11},{9,10},{10,... | collective-permute-start | bytes 147464 | tf_op jit(solution)/shard_map/ppermute | solution.py:589
  44.3 4.5 %collective-permute-start.16 = (bf16[48,512]{1,0:T(8,128)(2,1)S(1)}, bf16[48,512]{1,0:T(8,128)(2,1)S(1)}, u32[]{:S(2)}, u32[]{:S(2)}) collective-permute-start(bf16[48,512]{1,0:T(8,128)(2,1)S(1)} %get-tuple-element.70), channel_id=1, source_target_pairs={{0,4},{1,5},{2,6},{3,7},{4,0},{5,1},{6,2},{7,3},{8,12},{9,13},{10,... | collective-permute-start | bytes 147464 | tf_op jit(solution)/shard_map/ppermute | solution.py:632
  45.8 7.1 %collective-permute-start.17 = (bf16[48,512]{1,0:T(8,128)(2,1)S(1)}, bf16[48,512]{1,0:T(8,128)(2,1)S(1)}, u32[]{:S(2)}, u32[]{:S(2)}) collective-permute-start(bf16[48,512]{1,0:T(8,128)(2,1)S(1)} %get-tuple-element.71), channel_id=1, source_target_pairs={{0,8},{1,9},{2,10},{3,11},{4,12},{5,13},{6,14},{7,15},{8,0},{9,1},... | collective-permute-start | bytes 147464 | tf_op jit(solution)/shard_map/ppermute | solution.py:632
  46.8 6.1 %collective-permute-start.18 = (bf16[48,512]{1,0:T(8,128)(2,1)S(1)}, bf16[48,512]{1,0:T(8,128)(2,1)S(1)}, u32[]{:S(2)}, u32[]{:S(2)}) collective-permute-start(bf16[48,512]{1,0:T(8,128)(2,1)S(1)} %get-tuple-element.72), channel_id=1, source_target_pairs={{0,12},{1,13},{2,14},{3,15},{4,8},{5,9},{6,10},{7,11},{8,4},{9,5},... | collective-permute-start | bytes 147464 | tf_op jit(solution)/shard_map/ppermute | solution.py:632
  (1 other events, 1.0 us)

commit v2 on v1

--- a/solution.py
+++ b/solution.py
@@ -419,12 +419,6 @@
     return refs[0][...] if len(refs) == 1 else jnp.concatenate([ref[...] for ref in refs], axis=0)
 
 
-def next_kernel(mapped_ref, top_ref, total_ref, mixed_ref, *refs):
-    site_refs, outs = refs[:-3], refs[-3:]
-    held = top_ref[:, :1], total_ref[:, :1], mixed_ref[...]
-    keep(joined(held, scored(mapped_ref[...], sites_of(site_refs))), *outs)
-
-
 def late_kernel(mapped_ref, top_ref, total_ref, mixed_ref, map_ref, *refs, first, parts):
     site_refs, blocks = refs[:parts], refs[parts:]
     count = blocks[0].shape[0]
@@ -617,14 +611,14 @@
     near_parts, early = lax.optimization_barrier((near_parts, early))
     far_sites = join(near_parts)
     last_parts.append(swap(far_sites, 1))
-    held_sums = call(next_kernel, sums, [], [mapped, *early, far_sites], 2e8)
+    last_parts.append(far_sites)
 
     def late_blocks(first, after):
         return call(
             functools.partial(late_kernel, first=first, parts=len(last_parts)),
             [block] * (after - first),
             [],
-            [mapped, *held_sums, out_map, *last_parts],
+            [mapped, *early, out_map, *last_parts],
             3e8,
         )
 

time: 53.8 us -> 53.9 us (level)
  waiting for transfers between devices: 16.4 us -> 17.2 us
  Pallas kernels: 13.1 us -> 12.3 us
    ppermute x7, waiting for transfers between devices: 3.61 us -> 4.43 us  [swap(): return lax.ppermute(x, AXIS, [(d, d ^ bit) for d in range(devices)])]
    pallas_call x15 -> x14, Pallas kernels: 13.1 us -> 12.3 us  [call(): pl.pallas_call(kernel, out_shape=shapes, in_specs=[pl.BlockSpec(memory_sp...]
  transfers between devices with their start and end apart: 19 -> 19, of which waited for: 11 -> 11; matrix products, arithmetic and copies ran while one was open for 0% -> 0% of each run, Pallas kernels for 15% -> 14%
where the time goes in v2:
time: 53.9 us; the launch traced here: 53.7 us
  starting transfers between devices  21.4 us (40%)
  waiting for transfers between devices  17.2 us (32%)
  Pallas kernels  12.3 us (23%)
  local copies, waits for them, and re-layouts  2.51 us (5%)
    pallas_call x14, Pallas kernels, call(): pl.pallas_call(kernel, out_shape=shapes, in_specs=[pl.BlockSpec(memory_sp...  12.3 us
    ppermute x7, starting transfers between devices, swap(): return lax.ppermute(x, AXIS, [(d, d ^ bit) for d in range(devices)])  5.37 us
    ppermute x3, starting transfers between devices, per_device(): lax.ppermute(blocks[k], AXIS, turns[k])  5.11 us
    ppermute x3, waiting for transfers between devices, per_device(): lax.ppermute(blocks[k], AXIS, turns[k])  4.62 us
    ppermute x3, starting transfers between devices, per_device(): lax.ppermute(done[k], AXIS, turns[k])  4.45 us
    ppermute x7, waiting for transfers between devices, swap(): return lax.ppermute(x, AXIS, [(d, d ^ bit) for d in range(devices)])  4.43 us
    ppermute x3, waiting for transfers between devices, per_device(): lax.ppermute(done[k], AXIS, turns[k])  4.13 us
    ppermute x1, starting transfers between devices, per_device(): far_a = lax.ppermute(far_a, BOTH, outer)  2.64 us
  transfers between devices with their start and end apart: 19, of which 11 were waited for; matrix products, arithmetic and copies ran while one was open for 0% of the time, Pallas kernels for 14%

profile of v2, /device:TPU:0, one launch (start us, length us, event | category | flops | bytes accessed | tf_op | source)
XLA Modules:
  0.0 53.7 jit_solution(16410085098298740871)
XLA Ops:
  0.0 1.4 %copy-done = bf16[4,4,192,192]{3,2,1,0:T(8,128)(2,1)S(1)} copy-done((bf16[4,4,192,192]{3,2,1,0:T(8,128)(2,1)S(1)}, bf16[4,4,192,192]{3,2,1,0:T(8,128)(2,1)}, u32[]{:S(2)}) %copy-start) | copy-done | bytes 1179672
  1.4 1.0 %copy-done.4 = bf16[3,3,192,128]{3,2,1,0:T(8,128)(2,1)S(1)} copy-done((bf16[3,3,192,128]{3,2,1,0:T(8,128)(2,1)S(1)}, bf16[3,3,192,128]{3,2,1,0:T(8,128)(2,1)}, u32[]{:S(2)}) %copy-start.4) | copy-done | bytes 442392
  3.5 1.1 %collective-permute-done.2.near_ref = bf16[4,4,48,128]{3,2,1,0:T(8,128)(2,1)S(1)} collective-permute-done((bf16[4,4,48,128]{3,2,1,0:T(8,128)(2,1)S(1)}, bf16[4,4,48,128]{3,2,1,0:T(8,128)(2,1)S(1)}, u32[]{:S(2)}, u32[]{:S(2)}) %collective-permute-start.2) | collective-permute-done | bytes 196640 | tf_op jit(solution)/shard_map/ppermute | solution.py:529
  4.6 1.7 %shard_map.123.rest_ref = bf16[1,4,2,48,256]{4,3,2,1,0:T(8,128)(2,1)S(1)} custom-call(bf16[4,4,192,192]{3,2,1,0:T(8,128)(2,1)S(1)} %copy-done, bf16[3,3,192,128]{3,2,1,0:T(8,128)(2,1)S(1)} %copy-done.4, bf16[4,4,48,128]{3,2,1,0:T(8,128)(2,1)S(1)} %collective-permute-done.2.near_ref, bf16[3,128,128]{2,1,0:T(8,128)(2,1)S(1)} %copy-done.8, ...), custom_call_target="tpu_custom_call" | custom-call | flops 900000000 | bytes 2375680 | tf_op jit(solution)/shard_map/pallas_call | solution.py:455
  6.7 1.5 %shard_map.119 = bf16[2,4,48,128]{3,2,1,0:T(8,128)(2,1)S(1)} custom-call(bf16[4,4,192,192]{3,2,1,0:T(8,128)(2,1)} %video_ref.7, bf16[3,3,192,128]{3,2,1,0:T(8,128)(2,1)} %w_ref.10), custom_call_target="tpu_custom_call" | custom-call | flops 56623104 | bytes 1720320 | tf_op jit(solution)/shard_map/pallas_call | solution.py:455
  8.2 2.6 %collective-permute-start = (bf16[2,4,48,128]{3,2,1,0:T(8,128)(2,1)S(1)}, bf16[2,4,48,128]{3,2,1,0:T(8,128)(2,1)S(1)}, u32[]{:S(2)}, u32[]{:S(2)}) collective-permute-start(bf16[2,4,48,128]{3,2,1,0:T(8,128)(2,1)S(1)} %shard_map.119), channel_id=1, source_target_pairs={{1,2},{3,4},{5,6},{7,8},{9,10},{11,12},{13,14},{2,1},{4,3},{6,5},{... | collective-permute-start | bytes 294920 | tf_op jit(solution)/shard_map/ppermute | solution.py:523
  10.9 1.3 %shard_map.118 = (f32[4,4,48,128]{3,2,1,0:T(8,128)S(1)}, bf16[4,4,48,128]{3,2,1,0:T(8,128)(2,1)S(1)}) custom-call(bf16[4,4,192,192]{3,2,1,0:T(8,128)(2,1)S(1)} %copy-done.1, bf16[3,3,192,128]{3,2,1,0:T(8,128)(2,1)S(1)} %copy-done.5, bf16[3,128,128]{2,1,0:T(8,128)(2,1)S(1)} %copy-done.8), custom_call_target="tpu_custom_call" | custom-call | flops 566231040 | bytes 2310144 | tf_op jit(solution)/shard_map/pallas_call | solution.py:455
  12.2 1.2 %collective-permute-done.far_ref = bf16[2,4,48,128]{3,2,1,0:T(8,128)(2,1)S(1)} collective-permute-done((bf16[2,4,48,128]{3,2,1,0:T(8,128)(2,1)S(1)}, bf16[2,4,48,128]{3,2,1,0:T(8,128)(2,1)S(1)}, u32[]{:S(2)}, u32[]{:S(2)}) %collective-permute-start) | collective-permute-done | bytes 98336 | tf_op jit(solution)/shard_map/ppermute | solution.py:523
  13.8 2.1 %collective-permute-start.4 = (bf16[2,2,48,256]{3,2,1,0:T(8,128)(2,1)S(1)}, bf16[2,2,48,256]{3,2,1,0:T(8,128)(2,1)S(1)}, u32[]{:S(2)}, u32[]{:S(2)}) collective-permute-start(bf16[2,2,48,256]{3,2,1,0:T(8,128)(2,1)S(1)} %get-tuple-element.38.far_a_ref.d_ref), channel_id=1, source_target_pairs={{1,2},{3,4},{5,6},{7,8},{9,10},{11,12},{13,14},{2,1},{4,3},{6,5},{... | collective-permute-start | bytes 294920 | tf_op jit(solution)/shard_map/ppermute | solution.py:541
  16.4 0.7 %collective-permute-start.5 = (bf16[2,2,48,256]{3,2,1,0:T(8,128)(2,1)S(1)}, bf16[2,2,48,256]{3,2,1,0:T(8,128)(2,1)S(1)}, u32[]{:S(2)}, u32[]{:S(2)}) collective-permute-start(bf16[2,2,48,256]{3,2,1,0:T(8,128)(2,1)S(1)} %shard_map.122.far_b_ref.d_ref), channel_id=1, source_target_pairs={{1,2},{3,4},{5,6},{7,8},{9,10},{11,12},{13,14},{2,1},{4,3},{6,5},{... | collective-permute-start | bytes 294920 | tf_op jit(solution)/shard_map/ppermute | solution.py:559
  17.1 1.3 %shard_map.124 = (f32[4,2,48,256]{3,2,1,0:T(8,128)S(1)}, bf16[1,4,2,48,256]{4,3,2,1,0:T(8,128)(2,1)S(1)}) custom-call(bf16[2,2,48,256]{3,2,1,0:T(8,128)(2,1)S(1)} %get-tuple-element.38.far_a_ref.d_ref, bf16[2,2,48,256]{3,2,1,0:T(8,128)(2,1)S(1)} %shard_map.122.far_b_ref.d_ref, bf16[1,4,2,48,256]{4,3,2,1,0:T(8,128)(2,1)S(1)} %shard_map.123.rest_ref, ...), custom_call_target="tpu_custom_call" | custom-call | flops 900000000 | bytes 2752512 | tf_op jit(solution)/shard_map/pallas_call | solution.py:455
  18.5 0.8 %shard_map.125 = (bf16[2,1,48,512]{3,2,1,0:T(8,128)(2,1)S(1)}, bf16[2,2,48,256]{3,2,1,0:T(8,128)(2,1)S(1)}, bf16[2,1,48,512]{3,2,1,0:T(8,128)(2,1)S(1)}) custom-call(f32[4,2,48,256]{3,2,1,0:T(8,128)S(1)} %get-tuple-element.42.acc_ref, bf16[2,2,48,256]{3,2,1,0:T(8,128)(2,1)S(1)} %collective-permute-done.4.far_ref, ...), custom_call_target="tpu_custom_call" | custom-call | flops 300000000 | bytes 3703808 | tf_op jit(solution)/shard_map/pallas_call | solution.py:455
  19.3 1.8 %collective-permute-done.5.far_ref = bf16[2,2,48,256]{3,2,1,0:T(8,128)(2,1)S(1)} collective-permute-done((bf16[2,2,48,256]{3,2,1,0:T(8,128)(2,1)S(1)}, bf16[2,2,48,256]{3,2,1,0:T(8,128)(2,1)S(1)}, u32[]{:S(2)}, u32[]{:S(2)}) %collective-permute-start.5) | collective-permute-done | bytes 98336 | tf_op jit(solution)/shard_map/ppermute | solution.py:559
  21.1 1.0 %shard_map.126 = (bf16[2,1,48,512]{3,2,1,0:T(8,128)(2,1)S(1)}, bf16[48,512]{1,0:T(8,128)(2,1)S(1)}, bf16[48,512]{1,0:T(8,128)(2,1)S(1)}, bf16[48,512]{1,0:T(8,128)(2,1)S(1)}, bf16[48,512]{1,0:T(8,128)(2,1)S(1)}) custom-call(f32[4,2,48,256]{3,2,1,0:T(8,128)S(1)} %get-tuple-element.42.acc_ref, bf16[2,2,48,256]{3,2,1,0:T(8,128)(2,1)S(1)} %collective-permute-done.5.far_ref, ...), custom_call_target="tpu_custom_call" | custom-call | flops 300000000 | bytes 3900416 | tf_op jit(solution)/shard_map/pallas_call | solution.py:455
  22.1 4.5 %collective-permute-start.6 = (bf16[48,512]{1,0:T(8,128)(2,1)S(1)}, bf16[48,512]{1,0:T(8,128)(2,1)S(1)}, u32[]{:S(2)}, u32[]{:S(2)}) collective-permute-start(bf16[48,512]{1,0:T(8,128)(2,1)S(1)} %get-tuple-element.49), channel_id=1, source_target_pairs={{0,12},{1,13},{2,14},{3,15},{4,8},{5,9},{6,10},{7,11},{8,4},{9,5},... | collective-permute-start | bytes 147464 | tf_op jit(solution)/shard_map/ppermute | solution.py:589
  26.6 0.6 %collective-permute-start.8 = (bf16[48,512]{1,0:T(8,128)(2,1)S(1)}, bf16[48,512]{1,0:T(8,128)(2,1)S(1)}, u32[]{:S(2)}, u32[]{:S(2)}) collective-permute-start(bf16[48,512]{1,0:T(8,128)(2,1)S(1)} %get-tuple-element.51), channel_id=1, source_target_pairs={{0,8},{1,9},{2,10},{3,11},{4,12},{5,13},{6,14},{7,15},{8,0},{9,1},... | collective-permute-start | bytes 147464 | tf_op jit(solution)/shard_map/ppermute | solution.py:589
  27.2 1.9 %collective-permute-done.6 = bf16[48,512]{1,0:T(8,128)(2,1)S(1)} collective-permute-done((bf16[48,512]{1,0:T(8,128)(2,1)S(1)}, bf16[48,512]{1,0:T(8,128)(2,1)S(1)}, u32[]{:S(2)}, u32[]{:S(2)}) %collective-permute-start.6) | collective-permute-done | bytes 49184 | tf_op jit(solution)/shard_map/ppermute | solution.py:589
  29.1 1.7 %collective-permute-done.7 = bf16[48,512]{1,0:T(8,128)(2,1)S(1)} collective-permute-done((bf16[48,512]{1,0:T(8,128)(2,1)S(1)}, bf16[48,512]{1,0:T(8,128)(2,1)S(1)}, u32[]{:S(2)}, u32[]{:S(2)}) %collective-permute-start.7) | collective-permute-done | bytes 49184 | tf_op jit(solution)/shard_map/ppermute | solution.py:589
  30.8 1.0 %collective-permute-done.8 = bf16[48,512]{1,0:T(8,128)(2,1)S(1)} collective-permute-done((bf16[48,512]{1,0:T(8,128)(2,1)S(1)}, bf16[48,512]{1,0:T(8,128)(2,1)S(1)}, u32[]{:S(2)}, u32[]{:S(2)}) %collective-permute-start.8) | collective-permute-done | bytes 49184 | tf_op jit(solution)/shard_map/ppermute | solution.py:589
  31.9 1.4 %collective-permute-start.9 = (bf16[48,512]{1,0:T(8,128)(2,1)S(1)}, bf16[48,512]{1,0:T(8,128)(2,1)S(1)}, u32[]{:S(2)}, u32[]{:S(2)}) collective-permute-start(bf16[48,512]{1,0:T(8,128)(2,1)S(1)} %get-tuple-element.48), channel_id=1, source_target_pairs={{0,2},{1,3},{2,0},{3,1},{4,6},{5,7},{6,4},{7,5},{8,10},{9,11},{10,... | collective-permute-start | bytes 147464 | tf_op jit(solution)/shard_map/ppermute | solution.py:583
  33.3 0.7 %collective-permute-start.10 = (bf16[48,512]{1,0:T(8,128)(2,1)S(1)}, bf16[48,512]{1,0:T(8,128)(2,1)S(1)}, u32[]{:S(2)}, u32[]{:S(2)}) collective-permute-start(bf16[48,512]{1,0:T(8,128)(2,1)S(1)} %collective-permute-done.6), channel_id=1, source_target_pairs={{0,2},{1,3},{2,0},{3,1},{4,6},{5,7},{6,4},{7,5},{8,10},{9,11},{10,... | collective-permute-start | bytes 147464 | tf_op jit(solution)/shard_map/ppermute | solution.py:583
  33.9 1.4 %collective-permute-start.11 = (bf16[48,512]{1,0:T(8,128)(2,1)S(1)}, bf16[48,512]{1,0:T(8,128)(2,1)S(1)}, u32[]{:S(2)}, u32[]{:S(2)}) collective-permute-start(bf16[48,512]{1,0:T(8,128)(2,1)S(1)} %collective-permute-done.7), channel_id=1, source_target_pairs={{0,2},{1,3},{2,0},{3,1},{4,6},{5,7},{6,4},{7,5},{8,10},{9,11},{10,... | collective-permute-start | bytes 147464 | tf_op jit(solution)/shard_map/ppermute | solution.py:583
  35.3 0.7 %shard_map.127 = (bf16[512,512]{1,0:T(8,128)(2,1)S(1)}, bf16[512,512]{1,0:T(8,128)(2,1)S(1)}) custom-call(bf16[512,512]{1,0:T(8,128)(2,1)S(1)} %copy-done.9, bf16[512,512]{1,0:T(8,128)(2,1)S(1)} %copy-done.10, bf16[512,512]{1,0:T(8,128)(2,1)S(1)} %copy-done.11, bf16[512,512]{1,0:T(8,128)(2,1)S(1)} %copy-done.12), custom_call_target="tpu_custom_call" | custom-call | flops 500000000 | bytes 3145728 | tf_op jit(solution)/shard_map/pallas_call | solution.py:455
  38.2 1.4 %collective-permute-start.13 = (bf16[48,512]{1,0:T(8,128)(2,1)S(1)}, bf16[48,512]{1,0:T(8,128)(2,1)S(1)}, u32[]{:S(2)}, u32[]{:S(2)}) collective-permute-start(bf16[48,512]{1,0:T(8,128)(2,1)S(1)} %collective-permute-done.8), channel_id=1, source_target_pairs={{0,2},{1,3},{2,0},{3,1},{4,6},{5,7},{6,4},{7,5},{8,10},{9,11},{10,... | collective-permute-start | bytes 147464 | tf_op jit(solution)/shard_map/ppermute | solution.py:583
  40.1 2.3 %collective-permute-done.13.refs_0_ = bf16[48,512]{1,0:T(8,128)(2,1)S(1)} collective-permute-done((bf16[48,512]{1,0:T(8,128)(2,1)S(1)}, bf16[48,512]{1,0:T(8,128)(2,1)S(1)}, u32[]{:S(2)}, u32[]{:S(2)}) %collective-permute-start.13) | collective-permute-done | bytes 49184 | tf_op jit(solution)/shard_map/ppermute | solution.py:583
  42.4 0.9 %collective-permute-done.14.refs_1_ = bf16[48,512]{1,0:T(8,128)(2,1)S(1)} collective-permute-done((bf16[48,512]{1,0:T(8,128)(2,1)S(1)}, bf16[48,512]{1,0:T(8,128)(2,1)S(1)}, u32[]{:S(2)}, u32[]{:S(2)}) %collective-permute-start.14) | collective-permute-done | bytes 49184 | tf_op jit(solution)/shard_map/ppermute | solution.py:583
  43.4 1.0 %shard_map.130 = (bf16[48,512]{1,0:T(8,128)(2,1)S(1)}, bf16[48,512]{1,0:T(8,128)(2,1)S(1)}, bf16[48,512]{1,0:T(8,128)(2,1)S(1)}, bf16[48,512]{1,0:T(8,128)(2,1)S(1)}) custom-call(bf16[192,512]{1,0:T(8,128)(2,1)S(1)} %shard_map.128.mapped_ref, f32[192,128]{1,0:T(8,128)S(1)} %get-tuple-element.56.top_ref, f32[192,128]{1,0:T(8,128)S(1)} %get-tuple-element.57.total_ref, ...), custom_call_target="tpu_custom_call" | custom-call | flops 300000000 | bytes 1900544 | tf_op jit(solution)/shard_map/pallas_call | solution.py:455
  44.4 1.5 %collective-permute-start.16 = (bf16[48,512]{1,0:T(8,128)(2,1)S(1)}, bf16[48,512]{1,0:T(8,128)(2,1)S(1)}, u32[]{:S(2)}, u32[]{:S(2)}) collective-permute-start(bf16[48,512]{1,0:T(8,128)(2,1)S(1)} %get-tuple-element.64), channel_id=1, source_target_pairs={{0,4},{1,5},{2,6},{3,7},{4,0},{5,1},{6,2},{7,3},{8,12},{9,13},{10,... | collective-permute-start | bytes 147464 | tf_op jit(solution)/shard_map/ppermute | solution.py:626
  45.8 1.0 %collective-permute-start.17 = (bf16[48,512]{1,0:T(8,128)(2,1)S(1)}, bf16[48,512]{1,0:T(8,128)(2,1)S(1)}, u32[]{:S(2)}, u32[]{:S(2)}) collective-permute-start(bf16[48,512]{1,0:T(8,128)(2,1)S(1)} %get-tuple-element.65), channel_id=1, source_target_pairs={{0,8},{1,9},{2,10},{3,11},{4,12},{5,13},{6,14},{7,15},{8,0},{9,1},... | collective-permute-start | bytes 147464 | tf_op jit(solution)/shard_map/ppermute | solution.py:626
  46.9 2.0 %collective-permute-start.18 = (bf16[48,512]{1,0:T(8,128)(2,1)S(1)}, bf16[48,512]{1,0:T(8,128)(2,1)S(1)}, u32[]{:S(2)}, u32[]{:S(2)}) collective-permute-start(bf16[48,512]{1,0:T(8,128)(2,1)S(1)} %get-tuple-element.66), channel_id=1, source_target_pairs={{0,12},{1,13},{2,14},{3,15},{4,8},{5,9},{6,10},{7,11},{8,4},{9,5},... | collective-permute-start | bytes 147464 | tf_op jit(solution)/shard_map/ppermute | solution.py:626
  48.8 4.1 %collective-permute-done.17.refs_2_ = bf16[48,512]{1,0:T(8,128)(2,1)S(1)} collective-permute-done((bf16[48,512]{1,0:T(8,128)(2,1)S(1)}, bf16[48,512]{1,0:T(8,128)(2,1)S(1)}, u32[]{:S(2)}, u32[]{:S(2)}) %collective-permute-start.17) | collective-permute-done | bytes 49184 | tf_op jit(solution)/shard_map/ppermute | solution.py:626
  52.9 0.8 %shard_map.131 = bf16[4,1,48,512]{3,2,1,0:T(8,128)(2,1)} custom-call(bf16[2,1,48,512]{3,2,1,0:T(8,128)(2,1)S(1)} %get-tuple-element.44.a_ref, bf16[2,1,48,512]{3,2,1,0:T(8,128)(2,1)S(1)} %get-tuple-element.47.b_ref, bf16[48,512]{1,0:T(8,128)(2,1)S(1)} %get-tuple-element.63.refs_0_, bf16[48,512]{1,0:T(8,128)(2,1)S(1)} %collective-permute-done.16.refs_1_, ...), custom_call_target="tpu_custom_call" | custom-call | flops 1000000 | bytes 589824 | tf_op jit(solution)/shard_map/pallas_call | solution.py:455
  (56 shorter events, 5.1 us)
Async XLA Ops:
  0.0 1.4 %copy-start = (bf16[4,4,192,192]{3,2,1,0:T(8,128)(2,1)S(1)}, bf16[4,4,192,192]{3,2,1,0:T(8,128)(2,1)}, u32[]{:S(2)}) copy-start(bf16[4,4,192,192]{3,2,1,0:T(8,128)(2,1)} %video_ref.7) | copy-start | bytes 3538948
  2.4 2.2 %copy-start.7 = (bf16[2,2,128,256]{3,2,1,0:T(8,128)(2,1)S(1)}, bf16[2,2,128,256]{3,2,1,0:T(8,128)(2,1)}, u32[]{:S(2)}) copy-start(bf16[2,2,128,256]{3,2,1,0:T(8,128)(2,1)} %r_ref.7) | copy-start | bytes 786436
  2.4 2.2 %copy-start.8 = (bf16[3,128,128]{2,1,0:T(8,128)(2,1)S(1)}, bf16[3,128,128]{2,1,0:T(8,128)(2,1)}, u32[]{:S(2)}) copy-start(bf16[3,128,128]{2,1,0:T(8,128)(2,1)} %t_ref.10) | copy-start | bytes 294916
  3.0 1.6 %collective-permute-start.2 = (bf16[4,4,48,128]{3,2,1,0:T(8,128)(2,1)S(1)}, bf16[4,4,48,128]{3,2,1,0:T(8,128)(2,1)S(1)}, u32[]{:S(2)}, u32[]{:S(2)}) collective-permute-start(bf16[4,4,48,128]{3,2,1,0:T(8,128)(2,1)S(1)} %get-tuple-element.41), channel_id=1, source_target_pairs={{0,1},{1,0},{2,3},{3,2},{4,5},{5,4},{6,7},{7,6},{8,9},{9,8},{10,11... | collective-permute-start | bytes 589832 | tf_op jit(solution)/shard_map/ppermute | solution.py:529
  6.2 4.7 %copy-start.1 = (bf16[4,4,192,192]{3,2,1,0:T(8,128)(2,1)S(1)}, bf16[4,4,192,192]{3,2,1,0:T(8,128)(2,1)}, u32[]{:S(2)}) copy-start(bf16[4,4,192,192]{3,2,1,0:T(8,128)(2,1)} %video_ref.7) | copy-start | bytes 3538948
  6.3 4.7 %copy-start.5 = (bf16[3,3,192,128]{3,2,1,0:T(8,128)(2,1)S(1)}, bf16[3,3,192,128]{3,2,1,0:T(8,128)(2,1)}, u32[]{:S(2)}) copy-start(bf16[3,3,192,128]{3,2,1,0:T(8,128)(2,1)} %w_ref.10) | copy-start | bytes 1327108
  6.3 10.8 %collective-permute-start.3 = (bf16[4,2,48,256]{3,2,1,0:T(8,128)(2,1)S(1)}, bf16[4,2,48,256]{3,2,1,0:T(8,128)(2,1)S(1)}, u32[]{:S(2)}, u32[]{:S(2)}) collective-permute-start(bf16[4,2,48,256]{3,2,1,0:T(8,128)(2,1)S(1)} %bitcast.1), channel_id=1, source_target_pairs={{0,1},{1,0},{2,3},{3,2},{4,5},{5,4},{6,7},{7,6},{8,9},{9,8},{10,11... | collective-permute-start | bytes 589832 | tf_op jit(solution)/shard_map/ppermute | solution.py:551
  8.2 5.2 %collective-permute-start = (bf16[2,4,48,128]{3,2,1,0:T(8,128)(2,1)S(1)}, bf16[2,4,48,128]{3,2,1,0:T(8,128)(2,1)S(1)}, u32[]{:S(2)}, u32[]{:S(2)}) collective-permute-start(bf16[2,4,48,128]{3,2,1,0:T(8,128)(2,1)S(1)} %shard_map.119), channel_id=1, source_target_pairs={{1,2},{3,4},{5,6},{7,8},{9,10},{11,12},{13,14},{2,1},{4,3},{6,5},{... | collective-permute-start | bytes 294920 | tf_op jit(solution)/shard_map/ppermute | solution.py:523
  10.8 5.0 %copy-start.13 = (bf16[512]{0:T(512)(128)(2,1)S(1)}, bf16[512]{0:T(512)(128)(2,1)}, u32[]{:S(2)}) copy-start(bf16[512]{0:T(512)(128)(2,1)} %param.19) | copy-start | bytes 3076
  10.8 5.0 %collective-permute-start.1 = (bf16[2,4,48,128]{3,2,1,0:T(8,128)(2,1)S(1)}, bf16[2,4,48,128]{3,2,1,0:T(8,128)(2,1)S(1)}, u32[]{:S(2)}, u32[]{:S(2)}) collective-permute-start(bf16[2,4,48,128]{3,2,1,0:T(8,128)(2,1)S(1)} %get-tuple-element.39), channel_id=1, source_target_pairs={{1,2},{3,4},{5,6},{7,8},{9,10},{11,12},{13,14},{2,1},{4,3},{6,5},{... | collective-permute-start | bytes 294920 | tf_op jit(solution)/shard_map/ppermute | solution.py:528
  12.2 4.9 %copy-start.2 = (bf16[3,3,256,256]{3,2,1,0:T(8,128)(2,1)S(1)}, bf16[3,3,256,256]{3,2,1,0:T(8,128)(2,1)}, u32[]{:S(2)}) copy-start(bf16[3,3,256,256]{3,2,1,0:T(8,128)(2,1)} %w_ref.13) | copy-start | bytes 3538948
  12.2 4.9 %copy-start.6 = (bf16[3,256,256]{2,1,0:T(8,128)(2,1)S(1)}, bf16[3,256,256]{2,1,0:T(8,128)(2,1)}, u32[]{:S(2)}) copy-start(bf16[3,256,256]{2,1,0:T(8,128)(2,1)} %t_ref.13) | copy-start | bytes 1179652
  13.8 4.7 %collective-permute-start.4 = (bf16[2,2,48,256]{3,2,1,0:T(8,128)(2,1)S(1)}, bf16[2,2,48,256]{3,2,1,0:T(8,128)(2,1)S(1)}, u32[]{:S(2)}, u32[]{:S(2)}) collective-permute-start(bf16[2,2,48,256]{3,2,1,0:T(8,128)(2,1)S(1)} %get-tuple-element.38.far_a_ref.d_ref), channel_id=1, source_target_pairs={{1,2},{3,4},{5,6},{7,8},{9,10},{11,12},{13,14},{2,1},{4,3},{6,5},{... | collective-permute-start | bytes 294920 | tf_op jit(solution)/shard_map/ppermute | solution.py:541
  16.4 2.1 %copy-start.3 = (bf16[2,2,256,512]{3,2,1,0:T(8,128)(2,1)S(1)}, bf16[2,2,256,512]{3,2,1,0:T(8,128)(2,1)}, u32[]{:S(2)}) copy-start(bf16[2,2,256,512]{3,2,1,0:T(8,128)(2,1)} %r_ref.9) | copy-start | bytes 3145732
  16.4 4.7 %collective-permute-start.5 = (bf16[2,2,48,256]{3,2,1,0:T(8,128)(2,1)S(1)}, bf16[2,2,48,256]{3,2,1,0:T(8,128)(2,1)S(1)}, u32[]{:S(2)}, u32[]{:S(2)}) collective-permute-start(bf16[2,2,48,256]{3,2,1,0:T(8,128)(2,1)S(1)} %shard_map.122.far_b_ref.d_ref), channel_id=1, source_target_pairs={{1,2},{3,4},{5,6},{7,8},{9,10},{11,12},{13,14},{2,1},{4,3},{6,5},{... | collective-permute-start | bytes 294920 | tf_op jit(solution)/shard_map/ppermute | solution.py:559
  21.1 14.2 %copy-start.9 = (bf16[512,512]{1,0:T(8,128)(2,1)S(1)}, bf16[512,512]{1,0:T(8,128)(2,1)}, u32[]{:S(2)}) copy-start(bf16[512,512]{1,0:T(8,128)(2,1)} %q_ref.1) | copy-start | bytes 1572868
  21.1 14.2 %copy-start.10 = (bf16[512,512]{1,0:T(8,128)(2,1)S(1)}, bf16[512,512]{1,0:T(8,128)(2,1)}, u32[]{:S(2)}) copy-start(bf16[512,512]{1,0:T(8,128)(2,1)} %k_ref.1) | copy-start | bytes 1572868
  21.1 14.2 %copy-start.11 = (bf16[512,512]{1,0:T(8,128)(2,1)S(1)}, bf16[512,512]{1,0:T(8,128)(2,1)}, u32[]{:S(2)}) copy-start(bf16[512,512]{1,0:T(8,128)(2,1)} %v_ref.1) | copy-start | bytes 1572868
  21.1 14.2 %copy-start.12 = (bf16[512,512]{1,0:T(8,128)(2,1)S(1)}, bf16[512,512]{1,0:T(8,128)(2,1)}, u32[]{:S(2)}) copy-start(bf16[512,512]{1,0:T(8,128)(2,1)} %o_ref.1) | copy-start | bytes 1572868
  22.1 7.0 %collective-permute-start.6 = (bf16[48,512]{1,0:T(8,128)(2,1)S(1)}, bf16[48,512]{1,0:T(8,128)(2,1)S(1)}, u32[]{:S(2)}, u32[]{:S(2)}) collective-permute-start(bf16[48,512]{1,0:T(8,128)(2,1)S(1)} %get-tuple-element.49), channel_id=1, source_target_pairs={{0,12},{1,13},{2,14},{3,15},{4,8},{5,9},{6,10},{7,11},{8,4},{9,5},... | collective-permute-start | bytes 147464 | tf_op jit(solution)/shard_map/ppermute | solution.py:589
  26.6 4.2 %collective-permute-start.7 = (bf16[48,512]{1,0:T(8,128)(2,1)S(1)}, bf16[48,512]{1,0:T(8,128)(2,1)S(1)}, u32[]{:S(2)}, u32[]{:S(2)}) collective-permute-start(bf16[48,512]{1,0:T(8,128)(2,1)S(1)} %get-tuple-element.50), channel_id=1, source_target_pairs={{0,4},{1,5},{2,6},{3,7},{4,0},{5,1},{6,2},{7,3},{8,12},{9,13},{10,... | collective-permute-start | bytes 147464 | tf_op jit(solution)/shard_map/ppermute | solution.py:589
  26.6 5.3 %collective-permute-start.8 = (bf16[48,512]{1,0:T(8,128)(2,1)S(1)}, bf16[48,512]{1,0:T(8,128)(2,1)S(1)}, u32[]{:S(2)}, u32[]{:S(2)}) collective-permute-start(bf16[48,512]{1,0:T(8,128)(2,1)S(1)} %get-tuple-element.51), channel_id=1, source_target_pairs={{0,8},{1,9},{2,10},{3,11},{4,12},{5,13},{6,14},{7,15},{8,0},{9,1},... | collective-permute-start | bytes 147464 | tf_op jit(solution)/shard_map/ppermute | solution.py:589
  31.8 4.5 %collective-permute-start.12 = (bf16[192,512]{1,0:T(8,128)(2,1)S(1)}, bf16[192,512]{1,0:T(8,128)(2,1)S(1)}, u32[]{:S(2)}, u32[]{:S(2)}) collective-permute-start(bf16[192,512]{1,0:T(8,128)(2,1)S(1)} %constant_dynamic-update-slice_fusion.own_ref.refs_0_), channel_id=1, source_target_pairs={{0,1},{1,0},{2,3},{3,2},{4,5},{5,4},{6,7},{7,6},{8,9},{9,8},{10,11... | collective-permute-start | bytes 589832 | tf_op jit(solution)/shard_map/ppermute | solution.py:583
  31.9 5.1 %collective-permute-start.9 = (bf16[48,512]{1,0:T(8,128)(2,1)S(1)}, bf16[48,512]{1,0:T(8,128)(2,1)S(1)}, u32[]{:S(2)}, u32[]{:S(2)}) collective-permute-start(bf16[48,512]{1,0:T(8,128)(2,1)S(1)} %get-tuple-element.48), channel_id=1, source_target_pairs={{0,2},{1,3},{2,0},{3,1},{4,6},{5,7},{6,4},{7,5},{8,10},{9,11},{10,... | collective-permute-start | bytes 147464 | tf_op jit(solution)/shard_map/ppermute | solution.py:583
  33.3 4.3 %collective-permute-start.10 = (bf16[48,512]{1,0:T(8,128)(2,1)S(1)}, bf16[48,512]{1,0:T(8,128)(2,1)S(1)}, u32[]{:S(2)}, u32[]{:S(2)}) collective-permute-start(bf16[48,512]{1,0:T(8,128)(2,1)S(1)} %collective-permute-done.6), channel_id=1, source_target_pairs={{0,2},{1,3},{2,0},{3,1},{4,6},{5,7},{6,4},{7,5},{8,10},{9,11},{10,... | collective-permute-start | bytes 147464 | tf_op jit(solution)/shard_map/ppermute | solution.py:583
  33.9 4.2 %collective-permute-start.11 = (bf16[48,512]{1,0:T(8,128)(2,1)S(1)}, bf16[48,512]{1,0:T(8,128)(2,1)S(1)}, u32[]{:S(2)}, u32[]{:S(2)}) collective-permute-start(bf16[48,512]{1,0:T(8,128)(2,1)S(1)} %collective-permute-done.7), channel_id=1, source_target_pairs={{0,2},{1,3},{2,0},{3,1},{4,6},{5,7},{6,4},{7,5},{8,10},{9,11},{10,... | collective-permute-start | bytes 147464 | tf_op jit(solution)/shard_map/ppermute | solution.py:583
  38.2 5.2 %collective-permute-start.15 = (bf16[144,512]{1,0:T(8,128)(2,1)S(1)}, bf16[144,512]{1,0:T(8,128)(2,1)S(1)}, u32[]{:S(2)}, u32[]{:S(2)}) collective-permute-start(bf16[144,512]{1,0:T(8,128)(2,1)S(1)} %constant_dynamic-update-slice_fusion.4.refs_3_), channel_id=1, source_target_pairs={{0,1},{1,0},{2,3},{3,2},{4,5},{5,4},{6,7},{7,6},{8,9},{9,8},{10,11... | collective-permute-start | bytes 442376 | tf_op jit(solution)/shard_map/ppermute | solution.py:583
  38.2 4.2 %collective-permute-start.13 = (bf16[48,512]{1,0:T(8,128)(2,1)S(1)}, bf16[48,512]{1,0:T(8,128)(2,1)S(1)}, u32[]{:S(2)}, u32[]{:S(2)}) collective-permute-start(bf16[48,512]{1,0:T(8,128)(2,1)S(1)} %collective-permute-done.8), channel_id=1, source_target_pairs={{0,2},{1,3},{2,0},{3,1},{4,6},{5,7},{6,4},{7,5},{8,10},{9,11},{10,... | collective-permute-start | bytes 147464 | tf_op jit(solution)/shard_map/ppermute | solution.py:583
  39.6 3.7 %collective-permute-start.14 = (bf16[48,512]{1,0:T(8,128)(2,1)S(1)}, bf16[48,512]{1,0:T(8,128)(2,1)S(1)}, u32[]{:S(2)}, u32[]{:S(2)}) collective-permute-start(bf16[48,512]{1,0:T(8,128)(2,1)S(1)} %collective-permute-done.8), channel_id=1, source_target_pairs={{0,3},{1,2},{2,1},{3,0},{4,7},{5,6},{6,5},{7,4},{8,11},{9,10},{10,... | collective-permute-start | bytes 147464 | tf_op jit(solution)/shard_map/ppermute | solution.py:583
  44.4 4.5 %collective-permute-start.16 = (bf16[48,512]{1,0:T(8,128)(2,1)S(1)}, bf16[48,512]{1,0:T(8,128)(2,1)S(1)}, u32[]{:S(2)}, u32[]{:S(2)}) collective-permute-start(bf16[48,512]{1,0:T(8,128)(2,1)S(1)} %get-tuple-element.64), channel_id=1, source_target_pairs={{0,4},{1,5},{2,6},{3,7},{4,0},{5,1},{6,2},{7,3},{8,12},{9,13},{10,... | collective-permute-start | bytes 147464 | tf_op jit(solution)/shard_map/ppermute | solution.py:626
  45.8 7.1 %collective-permute-start.17 = (bf16[48,512]{1,0:T(8,128)(2,1)S(1)}, bf16[48,512]{1,0:T(8,128)(2,1)S(1)}, u32[]{:S(2)}, u32[]{:S(2)}) collective-permute-start(bf16[48,512]{1,0:T(8,128)(2,1)S(1)} %get-tuple-element.65), channel_id=1, source_target_pairs={{0,8},{1,9},{2,10},{3,11},{4,12},{5,13},{6,14},{7,15},{8,0},{9,1},... | collective-permute-start | bytes 147464 | tf_op jit(solution)/shard_map/ppermute | solution.py:626
  46.9 6.1 %collective-permute-start.18 = (bf16[48,512]{1,0:T(8,128)(2,1)S(1)}, bf16[48,512]{1,0:T(8,128)(2,1)S(1)}, u32[]{:S(2)}, u32[]{:S(2)}) collective-permute-start(bf16[48,512]{1,0:T(8,128)(2,1)S(1)} %get-tuple-element.66), channel_id=1, source_target_pairs={{0,12},{1,13},{2,14},{3,15},{4,8},{5,9},{6,10},{7,11},{8,4},{9,5},... | collective-permute-start | bytes 147464 | tf_op jit(solution)/shard_map/ppermute | solution.py:626
  (1 other events, 1.0 us)
